TPU v7x, 128 devices: a whole 4x4x4 slice. The times are simulated.
128 devices in a mesh: sub: 16 (over y, x), front: 8 (over z, core).
Axes of the slice: x: 4, y: 4, z: 4, core: 2. Of those that a mesh axis runs over, the one named last changes fastest.
Arguments:
- front_inverse: bfloat16 [16, 16384, 2048], P('sub', 'front'), may hold values from -0.75 to 0.75
- coupling: bfloat16 [16, 16384, 2048], P('sub', 'front'), may hold values from -0.0234375 to 0.0234375
- free_modes: bfloat16 [16, 300, 16384], P('sub', None, 'front'), may hold values from -0.09375 to 0.09375
- dof_offset: int32 [16, 256], P('sub', 'front'), may hold values from 0 to 2047, as said below
- interface_id: int32 [16, 256], replicated, may hold values from 0 to 2047, as said below
Outputs:
- attachment: bfloat16 [16, 256, 16384], P('sub', None, 'front')
- flexibility: float32 [2048, 2048], P(('sub', 'front'))
Inputs may be any that keep to these rules, and one draw needn't show every extreme that they name: `dof_offset`: within one substructure and one front the 32 offsets are distinct, and 0 and 2047 occur among them. `interface_id`: every value occurs exactly twice in the whole array.
All inputs are finite; a program needn't handle non-finite values.
Results may differ from a plain program's by a relative error of at most 0.02.
Values may be sent and summed in bfloat16 or wider, within the bound.
A program may use at most 128 MiB of HBM per device.

v0:
```python
import jax
import jax.numpy as jnp
from jax import lax
from jax.sharding import PartitionSpec as P


def shifted(value, axis, steps):
    count = lax.axis_size(axis)
    leading, last = (max(0, -steps), min(count, count - steps))
    return lax.ppermute(value, axis, [(source, source + steps) for source in range(leading, last)])


def contract_last(left, right):
    return lax.dot_general(
        left, right, (((1,), (1,)), ((), ())), preferred_element_type=jnp.float32
    )


def on_device(front_inverse, coupling, free_modes, dof_offset, interface_id):
    inverse_block = front_inverse[0]
    coupling_block = coupling[0]
    mode_block = free_modes[0]
    offsets = dof_offset[0]
    order = inverse_block.shape[0]
    columns_all = interface_id.shape[1]
    per_front = offsets.shape[0]
    fronts = lax.axis_size("front")
    front_pos = lax.axis_index("front")
    sub_pos = lax.axis_index("sub")
    column_ids = jnp.arange(columns_all, dtype=jnp.int32)
    local_ids = jnp.arange(per_front, dtype=jnp.int32)
    row_ids = jnp.arange(order, dtype=jnp.int32)
    column_pick = (column_ids[:, None] == front_pos * per_front + local_ids[None, :]).astype(
        jnp.float32
    )
    row_pick = (offsets[:, None] == row_ids[None, :]).astype(jnp.float32)
    forces = jnp.dot(column_pick, row_pick, precision=lax.Precision.HIGHEST)
    groups = 1
    width = columns_all // groups
    force_groups = forces.reshape(groups, width, order)
    moments = groups + fronts - 1

    def forward(moment, carry):
        solved, outgoing = carry
        incoming = shifted(outgoing, "front", 1)
        panel = moment - front_pos
        valid = (panel >= 0) & (panel < groups)
        clipped = jnp.clip(panel, 0, groups - 1)

        def forward_active(unused):
            load = lax.dynamic_index_in_dim(force_groups, clipped, 0, keepdims=False)
            reduced = (load - contract_last(incoming, coupling_block)).astype(jnp.bfloat16)
            return contract_last(reduced, inverse_block).astype(jnp.bfloat16)

        def forward_waiting(unused):
            return outgoing

        result = lax.cond(valid, forward_active, forward_waiting, 0)
        solved = lax.dynamic_update_index_in_dim(solved, result, clipped, 0)
        return (solved, result)

    forward_start = (
        jnp.zeros((groups, width, order), jnp.bfloat16),
        jnp.zeros((width, order), jnp.bfloat16),
    )
    solved, forward_last = lax.fori_loop(0, moments, forward, forward_start)

    def backward(moment, carry):
        moved, outgoing = carry
        incoming = shifted(outgoing, "front", -1)
        panel = moment - (fronts - 1 - front_pos)
        valid = (panel >= 0) & (panel < groups)
        clipped = jnp.clip(panel, 0, groups - 1)

        def backward_active(unused):
            upper = lax.dynamic_index_in_dim(solved, clipped, 0, keepdims=False).astype(jnp.float32)
            reduced = (upper - incoming.astype(jnp.float32)).astype(jnp.bfloat16)
            displaced = jnp.dot(reduced, inverse_block, preferred_element_type=jnp.float32)
            handed = jnp.dot(
                displaced.astype(jnp.bfloat16), coupling_block, preferred_element_type=jnp.float32
            )
            return (displaced, handed.astype(jnp.bfloat16))

        def backward_waiting(unused):
            return (lax.dynamic_index_in_dim(moved, clipped, 0, keepdims=False), outgoing)

        displaced, handed = lax.cond(valid, backward_active, backward_waiting, 0)
        moved = lax.dynamic_update_index_in_dim(moved, displaced, clipped, 0)
        return (moved, handed)

    backward_start = (
        jnp.zeros((groups, width, order), jnp.float32),
        jnp.zeros((width, order), jnp.bfloat16),
    )
    moved, backward_last = lax.fori_loop(0, moments, backward, backward_start)
    displacement = moved.reshape(columns_all, order)
    modal = lax.psum(
        contract_last(displacement.astype(jnp.bfloat16), mode_block).astype(jnp.bfloat16), "front"
    )
    deflated = displacement - jnp.dot(modal, mode_block, preferred_element_type=jnp.float32)
    own_rows = jnp.take(deflated, offsets, axis=1).T
    sub_labels = lax.dynamic_index_in_dim(interface_id, sub_pos, 0, keepdims=False)
    mine = lax.dynamic_slice_in_dim(sub_labels, front_pos * per_front, per_front)
    total_ids = interface_id.shape[0] * columns_all // 2
    dual_ids = jnp.arange(total_ids, dtype=jnp.int32)
    owners = lax.axis_size("sub") * fronts
    share = total_ids // owners
    placed = (sub_labels[:, None] == dual_ids[None, :]).astype(jnp.float32)
    spread = jnp.dot(own_rows, placed, precision=lax.Precision.HIGHEST)
    selector = (
        jnp.arange(share * lax.axis_size(("sub", "front")), dtype=jnp.int32)[:, None]
        == mine[None, :]
    ).astype(jnp.float32)
    flexibility = lax.psum_scatter(
        jnp.dot(selector, spread, precision=lax.Precision.HIGHEST),
        ("sub", "front"),
        scatter_dimension=0,
        tiled=True,
    )
    return (deflated.astype(jnp.bfloat16)[None], flexibility)


def solution(mesh):
    return jax.shard_map(
        on_device,
        mesh=mesh,
        in_specs=(
            P("sub", "front", None),
            P("sub", "front", None),
            P("sub", None, "front"),
            P("sub", "front"),
            P(),
        ),
        out_specs=(P("sub", None, "front"), P(("sub", "front"), None)),
        check_vma=False,
    )
```

profile of v0, /device:TPU:32, one launch (start us, length us, event | category | flops | bytes accessed | tf_op | source)
XLA Modules:
  0.0 1082.7 jit_solution(12320467952608244080)
XLA Ops:
  7.3 2.6 convolution_bitcast_fusion
  9.9 157.0 %while.35 = (s32[]{:T(128)}, bf16[1,256,2048]{2,1,0:T(8,128)(2,1)}, bf16[256,2048]{1,0:T(8,128)(2,1)S(1)}, s32[]{:T(128)}, f32[1,256,2048]{2,1,0:T(8,128)}, /*in...) while((s32[]{:T(128)}, bf16[1,256,2048]{2,1,0:T(8,128)(2,1)}, ...), condition=%wide.region_3.4_spmd, body=%wide.region_0.3_spmd.sunk | while | flops 4296540160 | bytes 33554680 | solution.py:66
  10.1 1.9 collective-permute-start
  12.0 14.2 %collective-permute-done = bf16[256,2048]{1,0:T(8,128)(2,1)S(1)} collective-permute-done((bf16[256,2048]{1,0:T(8,128)(2,1)S(1)}, bf16[256,2048]{1,0:T(8,128)(2,1)S(1)}, u32[]{:S(2)}, u32[]{:S(2)}) %collective-permute-start) | collective-permute-done | bytes 1048608 | tf_op jit(solution)/shard_map/while/body/eval_jaxpr/ppermute | solution.py:10
  27.3 1.9 collective-permute-start
  29.2 14.2 %collective-permute-done = bf16[256,2048]{1,0:T(8,128)(2,1)S(1)} collective-permute-done((bf16[256,2048]{1,0:T(8,128)(2,1)S(1)}, bf16[256,2048]{1,0:T(8,128)(2,1)S(1)}, u32[]{:S(2)}, u32[]{:S(2)}) %collective-permute-start) | collective-permute-done | bytes 1048608 | tf_op jit(solution)/shard_map/while/body/eval_jaxpr/ppermute | solution.py:10
  44.5 1.9 collective-permute-start
  46.4 22.7 %collective-permute-done = bf16[256,2048]{1,0:T(8,128)(2,1)S(1)} collective-permute-done((bf16[256,2048]{1,0:T(8,128)(2,1)S(1)}, bf16[256,2048]{1,0:T(8,128)(2,1)S(1)}, u32[]{:S(2)}, u32[]{:S(2)}) %collective-permute-start) | collective-permute-done | bytes 1048608 | tf_op jit(solution)/shard_map/while/body/eval_jaxpr/ppermute | solution.py:10
  69.0 10.9 %conditional.4 = (bf16[256,2048]{1,0:T(8,128)(2,1)S(1)}) conditional(s32[]{:T(128)} %convert_element_type.87, bf16[256,2048]{1,0:T(8,128)(2,1)S(1)} %copy.19, (f32[1,256,2048]{2,1,0:T(8,128)}, bf16[256,2048]{1,0:T(8,128)(2,1)S(1)}, bf16[2048,2048]{1,0:T(8,128)(2,1)}, bf16[2048,2048]{1,0:T(8,128)(2,1)}) %tuple.101), branch_computations={%region_1.1_spmd, %region_2.2_spmd} | conditional | flops 4296540160 | bytes 20971528 | solution.py:58
  69.0 10.9 %convolution_convert_fusion = bf16[256,2048]{1,0:T(8,128)(2,1)S(1)} fusion(bf16[2048,2048]{1,0:T(8,128)(2,1)} %get-tuple-element.340, bf16[256,2048]{1,0:T(8,128)(2,1)S(1)} %get-tuple-element.338, bf16[2048,2048]{1,0:T(8,128)(2,1)} %get-tuple-element.339, f32[1,256,2048]{2,1,0:T(8,128)} %get-tuple-element.337), kind=kOutput, calls=%fused_computation.3 | convolution fusion | flops 4296540160 | bytes 20971520 | tf_op jit(solution)/shard_map/while/body/eval_jaxpr/cond/branch_1_fun/dot_general | solution.py:14
  81.1 1.9 collective-permute-start
  83.0 14.2 %collective-permute-done = bf16[256,2048]{1,0:T(8,128)(2,1)S(1)} collective-permute-done((bf16[256,2048]{1,0:T(8,128)(2,1)S(1)}, bf16[256,2048]{1,0:T(8,128)(2,1)S(1)}, u32[]{:S(2)}, u32[]{:S(2)}) %collective-permute-start) | collective-permute-done | bytes 1048608 | tf_op jit(solution)/shard_map/while/body/eval_jaxpr/ppermute | solution.py:10
  98.3 1.9 collective-permute-start
  100.2 14.2 %collective-permute-done = bf16[256,2048]{1,0:T(8,128)(2,1)S(1)} collective-permute-done((bf16[256,2048]{1,0:T(8,128)(2,1)S(1)}, bf16[256,2048]{1,0:T(8,128)(2,1)S(1)}, u32[]{:S(2)}, u32[]{:S(2)}) %collective-permute-start) | collective-permute-done | bytes 1048608 | tf_op jit(solution)/shard_map/while/body/eval_jaxpr/ppermute | solution.py:10
  115.5 1.9 collective-permute-start
  117.4 14.2 %collective-permute-done = bf16[256,2048]{1,0:T(8,128)(2,1)S(1)} collective-permute-done((bf16[256,2048]{1,0:T(8,128)(2,1)S(1)}, bf16[256,2048]{1,0:T(8,128)(2,1)S(1)}, u32[]{:S(2)}, u32[]{:S(2)}) %collective-permute-start) | collective-permute-done | bytes 1048608 | tf_op jit(solution)/shard_map/while/body/eval_jaxpr/ppermute | solution.py:10
  132.6 9.8 collective-permute-start
  142.4 6.3 collective-permute-done
  149.8 9.8 collective-permute-start
  159.6 6.3 collective-permute-done
  167.1 1.6 broadcast_in_dim.51
  168.7 170.3 %while.36 = (s32[]{:T(128)}, f32[1,256,2048]{2,1,0:T(8,128)}, bf16[256,2048]{1,0:T(8,128)(2,1)S(1)}, s32[]{:T(128)}, bf16[1,256,2048]{2,1,0:T(8,128)(2,1)S(1)}, ...) while((s32[]{:T(128)}, f32[1,256,2048]{2,1,0:T(8,128)}, ...), condition=%wide.region_7.8_spmd, body=%wide.region_4.7_spmd.sunk | while | flops 4298113024 | bytes 70254896 | solution.py:95
  168.7 1.9 collective-permute-start.1
  170.6 12.3 %collective-permute-done.1 = bf16[256,2048]{1,0:T(8,128)(2,1)} collective-permute-done((bf16[256,2048]{1,0:T(8,128)(2,1)S(1)}, bf16[256,2048]{1,0:T(8,128)(2,1)}, u32[]{:S(2)}, u32[]{:S(2)}) %collective-permute-start.1) | collective-permute-done | bytes 1048608 | tf_op jit(solution)/shard_map/while/body/eval_jaxpr/ppermute | solution.py:10
  182.9 3.9 collective-permute-start.1
  186.8 12.3 %collective-permute-done.1 = bf16[256,2048]{1,0:T(8,128)(2,1)} collective-permute-done((bf16[256,2048]{1,0:T(8,128)(2,1)S(1)}, bf16[256,2048]{1,0:T(8,128)(2,1)}, u32[]{:S(2)}, u32[]{:S(2)}) %collective-permute-start.1) | collective-permute-done | bytes 1048608 | tf_op jit(solution)/shard_map/while/body/eval_jaxpr/ppermute | solution.py:10
  199.1 3.9 collective-permute-start.1
  203.0 12.3 %collective-permute-done.1 = bf16[256,2048]{1,0:T(8,128)(2,1)} collective-permute-done((bf16[256,2048]{1,0:T(8,128)(2,1)S(1)}, bf16[256,2048]{1,0:T(8,128)(2,1)}, u32[]{:S(2)}, u32[]{:S(2)}) %collective-permute-start.1) | collective-permute-done | bytes 1048608 | tf_op jit(solution)/shard_map/while/body/eval_jaxpr/ppermute | solution.py:10
  215.3 3.9 collective-permute-start.1
  219.2 12.3 %collective-permute-done.1 = bf16[256,2048]{1,0:T(8,128)(2,1)} collective-permute-done((bf16[256,2048]{1,0:T(8,128)(2,1)S(1)}, bf16[256,2048]{1,0:T(8,128)(2,1)}, u32[]{:S(2)}, u32[]{:S(2)}) %collective-permute-start.1) | collective-permute-done | bytes 1048608 | tf_op jit(solution)/shard_map/while/body/eval_jaxpr/ppermute | solution.py:10
  231.5 3.9 collective-permute-start.1
  235.4 12.3 %collective-permute-done.1 = bf16[256,2048]{1,0:T(8,128)(2,1)} collective-permute-done((bf16[256,2048]{1,0:T(8,128)(2,1)S(1)}, bf16[256,2048]{1,0:T(8,128)(2,1)}, u32[]{:S(2)}, u32[]{:S(2)}) %collective-permute-start.1) | collective-permute-done | bytes 1048608 | tf_op jit(solution)/shard_map/while/body/eval_jaxpr/ppermute | solution.py:10
  247.7 3.9 collective-permute-start.1
  251.7 39.7 %collective-permute-done.1 = bf16[256,2048]{1,0:T(8,128)(2,1)} collective-permute-done((bf16[256,2048]{1,0:T(8,128)(2,1)S(1)}, bf16[256,2048]{1,0:T(8,128)(2,1)}, u32[]{:S(2)}, u32[]{:S(2)}) %collective-permute-start.1) | collective-permute-done | bytes 1048608 | tf_op jit(solution)/shard_map/while/body/eval_jaxpr/ppermute | solution.py:10
  291.4 8.5 conditional.5
  291.4 6.2 fusion.2
  297.6 2.3 convolution_convert_fusion.1
  300.0 1.9 collective-permute-start.1
  301.9 12.3 %collective-permute-done.1 = bf16[256,2048]{1,0:T(8,128)(2,1)} collective-permute-done((bf16[256,2048]{1,0:T(8,128)(2,1)S(1)}, bf16[256,2048]{1,0:T(8,128)(2,1)}, u32[]{:S(2)}, u32[]{:S(2)}) %collective-permute-start.1) | collective-permute-done | bytes 1048608 | tf_op jit(solution)/shard_map/while/body/eval_jaxpr/ppermute | solution.py:10
  314.2 12.5 %collective-permute-start.1 = (bf16[256,2048]{1,0:T(8,128)(2,1)S(1)}, bf16[256,2048]{1,0:T(8,128)(2,1)}, u32[]{:S(2)}, u32[]{:S(2)}) collective-permute-start(bf16[256,2048]{1,0:T(8,128)(2,1)S(1)} %get-tuple-element.526), channel_id=1, source_target_pairs={{1,0},{2,1},{3,2},{4,3},{5,4},{6,5},{7,6},{9,8},{10,9},{11,10},{12... | collective-permute-start | bytes 3145736 | tf_op jit(solution)/shard_map/while/body/eval_jaxpr/ppermute | solution.py:10
  326.7 12.3 %collective-permute-done.1 = bf16[256,2048]{1,0:T(8,128)(2,1)} collective-permute-done((bf16[256,2048]{1,0:T(8,128)(2,1)S(1)}, bf16[256,2048]{1,0:T(8,128)(2,1)}, u32[]{:S(2)}, u32[]{:S(2)}) %collective-permute-start.1) | collective-permute-done | bytes 1048608 | tf_op jit(solution)/shard_map/while/body/eval_jaxpr/ppermute | solution.py:10
  339.0 3.1 fusion.10
  343.9 56.5 %all-reduce.2.cloned.1.call-done = bf16[256,300]{1,0:T(8,128)(2,1)} async-done(((bf16[256,300]{1,0:T(8,128)(2,1)}), bf16[256,300]{1,0:T(8,128)(2,1)}) %all-reduce.2.cloned.1.call-update) | async-done | bytes 153616 | tf_op jit(solution)/shard_map/psum | solution.py:97
  400.5 3.0 convolution_subtract_fusion.1
  403.5 1.9 copy.7
  406.9 9.5 fusion.16
  416.5 1.6 copy-done.5
  419.2 656.7 %reduce-scatter.2.cloned.1.call-done = f32[16,2048]{1,0:T(8,128)} async-done(((f32[2048,2048]{1,0:T(8,128)}), f32[16,2048]{1,0:T(8,128)}) %reduce-scatter.2.cloned.1.call-update) | async-done | bytes 131088 | tf_op jit(solution)/shard_map/reduce_scatter | solution.py:114
  (75 shorter events, 13.2 us)
Async XLA Ops:
  7.2 331.8 %copy-start = (bf16[1,300,2048]{2,1,0:T(8,128)(2,1)S(1)}, bf16[1,300,2048]{2,1,0:T(8,128)(2,1)}, u32[]{:S(2)}) copy-start(bf16[1,300,2048]{2,1,0:T(8,128)(2,1)} %param.15) | copy-start | bytes 3686404
  7.2 393.3 %all-reduce.2.cloned.1.call-start = ((), (), s32[]{:S(2)}) async-start(), calls=%async_computation.1 | async-start | bytes 393216 | tf_op jit(solution)/shard_map/psum | solution.py:97
  10.1 16.1 %collective-permute-start = (bf16[256,2048]{1,0:T(8,128)(2,1)S(1)}, bf16[256,2048]{1,0:T(8,128)(2,1)S(1)}, u32[]{:S(2)}, u32[]{:S(2)}) collective-permute-start(bf16[256,2048]{1,0:T(8,128)(2,1)S(1)} %copy.19), channel_id=1, source_target_pairs={{0,1},{1,2},{2,3},{3,4},{4,5},{5,6},{6,7},{8,9},{9,10},{10,11},{11... | collective-permute-start | bytes 3145736 | tf_op jit(solution)/shard_map/while/body/eval_jaxpr/ppermute | solution.py:10
  26.2 1.0 copy-start.1
  27.3 16.1 %collective-permute-start = (bf16[256,2048]{1,0:T(8,128)(2,1)S(1)}, bf16[256,2048]{1,0:T(8,128)(2,1)S(1)}, u32[]{:S(2)}, u32[]{:S(2)}) collective-permute-start(bf16[256,2048]{1,0:T(8,128)(2,1)S(1)} %copy.19), channel_id=1, source_target_pairs={{0,1},{1,2},{2,3},{3,4},{4,5},{5,6},{6,7},{8,9},{9,10},{10,11},{11... | collective-permute-start | bytes 3145736 | tf_op jit(solution)/shard_map/while/body/eval_jaxpr/ppermute | solution.py:10
  43.4 1.0 copy-start.1
  44.5 24.6 %collective-permute-start = (bf16[256,2048]{1,0:T(8,128)(2,1)S(1)}, bf16[256,2048]{1,0:T(8,128)(2,1)S(1)}, u32[]{:S(2)}, u32[]{:S(2)}) collective-permute-start(bf16[256,2048]{1,0:T(8,128)(2,1)S(1)} %copy.19), channel_id=1, source_target_pairs={{0,1},{1,2},{2,3},{3,4},{4,5},{5,6},{6,7},{8,9},{9,10},{10,11},{11... | collective-permute-start | bytes 3145736 | tf_op jit(solution)/shard_map/while/body/eval_jaxpr/ppermute | solution.py:10
  80.0 1.0 copy-start.1
  81.1 16.1 %collective-permute-start = (bf16[256,2048]{1,0:T(8,128)(2,1)S(1)}, bf16[256,2048]{1,0:T(8,128)(2,1)S(1)}, u32[]{:S(2)}, u32[]{:S(2)}) collective-permute-start(bf16[256,2048]{1,0:T(8,128)(2,1)S(1)} %copy.19), channel_id=1, source_target_pairs={{0,1},{1,2},{2,3},{3,4},{4,5},{5,6},{6,7},{8,9},{9,10},{10,11},{11... | collective-permute-start | bytes 3145736 | tf_op jit(solution)/shard_map/while/body/eval_jaxpr/ppermute | solution.py:10
  97.2 1.0 copy-start.1
  98.3 16.1 %collective-permute-start = (bf16[256,2048]{1,0:T(8,128)(2,1)S(1)}, bf16[256,2048]{1,0:T(8,128)(2,1)S(1)}, u32[]{:S(2)}, u32[]{:S(2)}) collective-permute-start(bf16[256,2048]{1,0:T(8,128)(2,1)S(1)} %copy.19), channel_id=1, source_target_pairs={{0,1},{1,2},{2,3},{3,4},{4,5},{5,6},{6,7},{8,9},{9,10},{10,11},{11... | collective-permute-start | bytes 3145736 | tf_op jit(solution)/shard_map/while/body/eval_jaxpr/ppermute | solution.py:10
  114.4 1.0 copy-start.1
  115.5 16.1 %collective-permute-start = (bf16[256,2048]{1,0:T(8,128)(2,1)S(1)}, bf16[256,2048]{1,0:T(8,128)(2,1)S(1)}, u32[]{:S(2)}, u32[]{:S(2)}) collective-permute-start(bf16[256,2048]{1,0:T(8,128)(2,1)S(1)} %copy.19), channel_id=1, source_target_pairs={{0,1},{1,2},{2,3},{3,4},{4,5},{5,6},{6,7},{8,9},{9,10},{10,11},{11... | collective-permute-start | bytes 3145736 | tf_op jit(solution)/shard_map/while/body/eval_jaxpr/ppermute | solution.py:10
  131.6 1.0 copy-start.1
  132.6 16.1 %collective-permute-start = (bf16[256,2048]{1,0:T(8,128)(2,1)S(1)}, bf16[256,2048]{1,0:T(8,128)(2,1)S(1)}, u32[]{:S(2)}, u32[]{:S(2)}) collective-permute-start(bf16[256,2048]{1,0:T(8,128)(2,1)S(1)} %copy.19), channel_id=1, source_target_pairs={{0,1},{1,2},{2,3},{3,4},{4,5},{5,6},{6,7},{8,9},{9,10},{10,11},{11... | collective-permute-start | bytes 3145736 | tf_op jit(solution)/shard_map/while/body/eval_jaxpr/ppermute | solution.py:10
  148.8 1.0 copy-start.1
  149.8 16.1 %collective-permute-start = (bf16[256,2048]{1,0:T(8,128)(2,1)S(1)}, bf16[256,2048]{1,0:T(8,128)(2,1)S(1)}, u32[]{:S(2)}, u32[]{:S(2)}) collective-permute-start(bf16[256,2048]{1,0:T(8,128)(2,1)S(1)} %copy.19), channel_id=1, source_target_pairs={{0,1},{1,2},{2,3},{3,4},{4,5},{5,6},{6,7},{8,9},{9,10},{10,11},{11... | collective-permute-start | bytes 3145736 | tf_op jit(solution)/shard_map/while/body/eval_jaxpr/ppermute | solution.py:10
  166.0 1.0 copy-start.1
  166.9 1.7 copy-start.2
  168.7 14.2 %collective-permute-start.1 = (bf16[256,2048]{1,0:T(8,128)(2,1)S(1)}, bf16[256,2048]{1,0:T(8,128)(2,1)}, u32[]{:S(2)}, u32[]{:S(2)}) collective-permute-start(bf16[256,2048]{1,0:T(8,128)(2,1)S(1)} %get-tuple-element.526), channel_id=1, source_target_pairs={{1,0},{2,1},{3,2},{4,3},{5,4},{6,5},{7,6},{9,8},{10,9},{11,10},{12... | collective-permute-start | bytes 3145736 | tf_op jit(solution)/shard_map/while/body/eval_jaxpr/ppermute | solution.py:10
  182.9 16.2 %collective-permute-start.1 = (bf16[256,2048]{1,0:T(8,128)(2,1)S(1)}, bf16[256,2048]{1,0:T(8,128)(2,1)}, u32[]{:S(2)}, u32[]{:S(2)}) collective-permute-start(bf16[256,2048]{1,0:T(8,128)(2,1)S(1)} %get-tuple-element.526), channel_id=1, source_target_pairs={{1,0},{2,1},{3,2},{4,3},{5,4},{6,5},{7,6},{9,8},{10,9},{11,10},{12... | collective-permute-start | bytes 3145736 | tf_op jit(solution)/shard_map/while/body/eval_jaxpr/ppermute | solution.py:10
  199.1 16.2 %collective-permute-start.1 = (bf16[256,2048]{1,0:T(8,128)(2,1)S(1)}, bf16[256,2048]{1,0:T(8,128)(2,1)}, u32[]{:S(2)}, u32[]{:S(2)}) collective-permute-start(bf16[256,2048]{1,0:T(8,128)(2,1)S(1)} %get-tuple-element.526), channel_id=1, source_target_pairs={{1,0},{2,1},{3,2},{4,3},{5,4},{6,5},{7,6},{9,8},{10,9},{11,10},{12... | collective-permute-start | bytes 3145736 | tf_op jit(solution)/shard_map/while/body/eval_jaxpr/ppermute | solution.py:10
  215.3 16.2 %collective-permute-start.1 = (bf16[256,2048]{1,0:T(8,128)(2,1)S(1)}, bf16[256,2048]{1,0:T(8,128)(2,1)}, u32[]{:S(2)}, u32[]{:S(2)}) collective-permute-start(bf16[256,2048]{1,0:T(8,128)(2,1)S(1)} %get-tuple-element.526), channel_id=1, source_target_pairs={{1,0},{2,1},{3,2},{4,3},{5,4},{6,5},{7,6},{9,8},{10,9},{11,10},{12... | collective-permute-start | bytes 3145736 | tf_op jit(solution)/shard_map/while/body/eval_jaxpr/ppermute | solution.py:10
  231.5 16.2 %collective-permute-start.1 = (bf16[256,2048]{1,0:T(8,128)(2,1)S(1)}, bf16[256,2048]{1,0:T(8,128)(2,1)}, u32[]{:S(2)}, u32[]{:S(2)}) collective-permute-start(bf16[256,2048]{1,0:T(8,128)(2,1)S(1)} %get-tuple-element.526), channel_id=1, source_target_pairs={{1,0},{2,1},{3,2},{4,3},{5,4},{6,5},{7,6},{9,8},{10,9},{11,10},{12... | collective-permute-start | bytes 3145736 | tf_op jit(solution)/shard_map/while/body/eval_jaxpr/ppermute | solution.py:10
  247.7 43.7 %collective-permute-start.1 = (bf16[256,2048]{1,0:T(8,128)(2,1)S(1)}, bf16[256,2048]{1,0:T(8,128)(2,1)}, u32[]{:S(2)}, u32[]{:S(2)}) collective-permute-start(bf16[256,2048]{1,0:T(8,128)(2,1)S(1)} %get-tuple-element.526), channel_id=1, source_target_pairs={{1,0},{2,1},{3,2},{4,3},{5,4},{6,5},{7,6},{9,8},{10,9},{11,10},{12... | collective-permute-start | bytes 3145736 | tf_op jit(solution)/shard_map/while/body/eval_jaxpr/ppermute | solution.py:10
  291.4 6.2 copy-start.7
  297.6 2.4 copy-start.3
  300.0 14.2 %collective-permute-start.1 = (bf16[256,2048]{1,0:T(8,128)(2,1)S(1)}, bf16[256,2048]{1,0:T(8,128)(2,1)}, u32[]{:S(2)}, u32[]{:S(2)}) collective-permute-start(bf16[256,2048]{1,0:T(8,128)(2,1)S(1)} %get-tuple-element.526), channel_id=1, source_target_pairs={{1,0},{2,1},{3,2},{4,3},{5,4},{6,5},{7,6},{9,8},{10,9},{11,10},{12... | collective-permute-start | bytes 3145736 | tf_op jit(solution)/shard_map/while/body/eval_jaxpr/ppermute | solution.py:10
  314.2 24.8 %collective-permute-start.1 = (bf16[256,2048]{1,0:T(8,128)(2,1)S(1)}, bf16[256,2048]{1,0:T(8,128)(2,1)}, u32[]{:S(2)}, u32[]{:S(2)}) collective-permute-start(bf16[256,2048]{1,0:T(8,128)(2,1)S(1)} %get-tuple-element.526), channel_id=1, source_target_pairs={{1,0},{2,1},{3,2},{4,3},{5,4},{6,5},{7,6},{9,8},{10,9},{11,10},{12... | collective-permute-start | bytes 3145736 | tf_op jit(solution)/shard_map/while/body/eval_jaxpr/ppermute | solution.py:10
  339.0 3.4 copy-start.6
  339.0 61.5 %copy-start.4 = (f32[1,256,2048]{2,1,0:T(8,128)S(1)}, f32[1,256,2048]{2,1,0:T(8,128)}, u32[]{:S(2)}) copy-start(f32[1,256,2048]{2,1,0:T(8,128)} %get-tuple-element.367) | copy-start | bytes 6291460
  342.2 733.7 %reduce-scatter.2.cloned.1.call-start = ((), (), s32[]{:S(2)}) async-start(), calls=%async_computation.2 | async-start | bytes 16908288 | tf_op jit(solution)/shard_map/reduce_scatter | solution.py:114
  416.5 1.6 copy-start.5
Sparse Core Ops, SparseCore 0:
  342.3 58.1 all-reduce.1
  416.6 659.1 reduce-scatter.1
where the time goes:
time: 1090 us; the launch traced here: 1080 us
  waiting for transfers between devices  945 us (87%)
  starting transfers between devices  67.2 us (6%)
  matrix products  38.6 us (4%)
  local copies, waits for them, and re-layouts  15.9 us (1%)
  between operations  14.1 us (1%)
    reduce_scatter x1, waiting for transfers between devices, on_device(): lax.psum_scatter(jnp.dot(selector, spread, precision=lax.Precision.HIGHES...  657 us
    ppermute x16, waiting for transfers between devices, shifted(): lax.ppermute(value, axis, [(source, source + steps) for source in range(l...  232 us
    ppermute x16, starting transfers between devices, shifted(): lax.ppermute(value, axis, [(source, source + steps) for source in range(l...  66.9 us
    psum x1, waiting for transfers between devices, on_device(): lax.psum(contract_last(displacement.astype(jnp.bfloat16), mode_block).ast...  56.5 us
  transfers between devices with their start and end apart: 18, of which 18 were waited for; matrix products, arithmetic and copies ran while one was open for 0% of the time, Pallas kernels for 0%

commit v1 on v0

v1 whole, which is shorter than its diff:
```python
import functools

import jax
import jax.numpy as jnp
from jax import lax
from jax.experimental import pallas as pl
from jax.experimental.pallas import tpu as pltpu
from jax.sharding import PartitionSpec as P

MESH = pl.DeviceIdType.MESH
F32 = jnp.float32
BF16 = jnp.bfloat16

FRONTS = 8
SUBS = 16
NF = 2048
COLS = 256
OWN = 32
GROUPS = 4
WIDTH = 64
MODES = 300
MPAD = 384
SHARE = 16
HIGH = 5


def dot(left, right):
    return jnp.dot(left, right, preferred_element_type=F32)


def dot_last(left, right):
    return lax.dot_general(left, right, (((1,), (1,)), ((), ())), preferred_element_type=F32)


def tile(index, size):
    return pl.ds(pl.multiple_of(index * size, size), size)


def kernel(
    inverse_hbm,
    coupling_hbm,
    modes_hbm,
    offsets_ref,
    ids_ref,
    attachment_hbm,
    flexibility_hbm,
    inverse,
    coupling,
    modes_raw,
    modes,
    product,
    turned,
    coupling_turned,
    modal_map,
    pick,
    own,
    solved,
    solved_in,
    back,
    handed,
    handed_in,
    modal_out,
    modal_in,
    modal,
    mode_rows,
    entries,
    route,
    rows_out,
    rows_in,
    low_pick,
    displaced,
    attachment,
    flexibility,
    load_sem,
    fwd_send,
    fwd_recv,
    bwd_send,
    bwd_recv,
    sum_send,
    sum_recv,
    modal_send,
    modal_recv,
    mode_send,
    mode_recv,
    entry_send,
    entry_recv,
    row_send,
    row_recv,
    store_sem,
):
    front = lax.axis_index("front")
    sub = lax.axis_index("sub")
    high = front >= HIGH
    low = jnp.logical_and(front >= 1, front < HIGH)

    loads = [
        pltpu.make_async_copy(inverse_hbm.at[0], inverse, load_sem.at[0]),
        pltpu.make_async_copy(coupling_hbm.at[0], coupling, load_sem.at[1]),
        pltpu.make_async_copy(modes_hbm.at[0], modes_raw, load_sem.at[2]),
    ]
    for load in loads:
        load.start()

    def peer_front(step):
        return lax.rem(front + step, FRONTS)

    def peer_sub(step):
        return lax.rem(sub + step, SUBS)

    barrier = pltpu.get_barrier_semaphore()

    def greet_front(step, carry):
        pl.semaphore_signal(barrier, inc=1, device_id={"front": peer_front(step)}, device_id_type=MESH)
        return carry

    def greet_sub(step, carry):
        pl.semaphore_signal(barrier, inc=1, device_id={"sub": peer_sub(step)}, device_id_type=MESH)
        return carry

    lax.fori_loop(1, FRONTS, greet_front, 0)
    lax.fori_loop(1, SUBS, greet_sub, 0)

    offsets_square = jnp.broadcast_to(offsets_ref[...].astype(F32), (OWN, OWN))
    diagonal = lax.broadcasted_iota(jnp.int32, (OWN, OWN), 0) == lax.broadcasted_iota(
        jnp.int32, (OWN, OWN), 1
    )
    offsets_column = jnp.sum(
        jnp.where(diagonal, offsets_square, 0.0), axis=1, keepdims=True
    ).astype(jnp.int32)
    pick[...] = (offsets_column == lax.broadcasted_iota(jnp.int32, (OWN, NF), 1)).astype(F32).astype(BF16)
    place = lax.broadcasted_iota(jnp.int32, (COLS, COLS), 0)
    target = lax.shift_right_logical(place, 4) * (FRONTS * SHARE) + jnp.bitwise_and(place, 15) + front * SHARE
    route[...] = (target == ids_ref[pl.ds(sub, 1), :]).astype(F32).astype(BF16)
    lane_place = lax.broadcasted_iota(jnp.int32, (128, COLS), 0)

    def fill_low(index, carry):
        ids = jnp.bitwise_and(ids_ref[pl.ds(index, 1), :], 127)
        low_pick[index] = (lane_place == ids).astype(F32).astype(BF16)
        return carry

    lax.fori_loop(0, SUBS, fill_low, 0)
    solved[...] = jnp.zeros((COLS, NF), BF16)
    modes[...] = jnp.zeros((MPAD, NF), BF16)

    pl.semaphore_wait(barrier, FRONTS - 1 + SUBS - 1)

    def turn(source, destination):
        def one(index, carry):
            destination[:, tile(index, 512)] = source[tile(index, 512), :].T
            return carry

        lax.fori_loop(0, NF // 512, one, 0)

    loads[0].wait()

    @pl.when(jnp.logical_not(low))
    def _():
        def one(index, carry):
            own[:, tile(index, 512)] = dot_last(pick[...], inverse[tile(index, 512), :]).astype(BF16)
            return carry

        lax.fori_loop(0, NF // 512, one, 0)

    @pl.when(low)
    def _():
        turn(inverse, turned)

    loads[1].wait()

    @pl.when(low)
    def _():
        turn(coupling, coupling_turned)

        def one(index, carry):
            own[:, tile(index, 512)] = dot(pick[...], turned[:, tile(index, 512)]).astype(BF16)
            return carry

        lax.fori_loop(0, NF // 512, one, 0)

    own_start = pl.multiple_of(front * OWN, OWN)
    own_rows = pl.ds(own_start, OWN)
    solved[own_rows, :] = own[...]

    def copy_fwd(group):
        return pltpu.make_async_remote_copy(
            src_ref=solved.at[tile(group, WIDTH)],
            dst_ref=solved_in.at[group],
            send_sem=fwd_send.at[group],
            recv_sem=fwd_recv.at[group],
            device_id={"front": jnp.minimum(front + 1, FRONTS - 1)},
            device_id_type=MESH,
        )

    def copy_bwd(group):
        return pltpu.make_async_remote_copy(
            src_ref=handed.at[group],
            dst_ref=handed_in.at[group],
            send_sem=bwd_send.at[group],
            recv_sem=bwd_recv.at[group],
            device_id={"front": jnp.maximum(front - 1, 0)},
            device_id_type=MESH,
        )

    def copy_sum(group):
        return pltpu.make_async_remote_copy(
            src_ref=modal_out.at[group],
            dst_ref=modal_in.at[group],
            send_sem=sum_send.at[group],
            recv_sem=sum_recv.at[group],
            device_id={"front": jnp.maximum(front - 1, 0)},
            device_id_type=MESH,
        )

    def copy_modal(group, step):
        return pltpu.make_async_remote_copy(
            src_ref=modal.at[tile(group, WIDTH)],
            dst_ref=modal.at[tile(group, WIDTH)],
            send_sem=modal_send.at[group, step],
            recv_sem=modal_recv.at[group],
            device_id={"front": peer_front(step)},
            device_id_type=MESH,
        )

    def rows_of(buffer, sends, receives, step, index):
        rows = pl.ds(pl.multiple_of(index * OWN, OWN), OWN)
        return pltpu.make_async_remote_copy(
            src_ref=buffer.at[rows],
            dst_ref=buffer.at[rows],
            send_sem=sends.at[step],
            recv_sem=receives.at[index],
            device_id={"front": peer_front(step)},
            device_id_type=MESH,
        )

    def copy_mode(step, index):
        return rows_of(mode_rows, mode_send, mode_recv, step, index)

    def copy_entry(step, index):
        return rows_of(entries, entry_send, entry_recv, step, index)

    def copy_row(step, source):
        return pltpu.make_async_remote_copy(
            src_ref=rows_out.at[peer_sub(step)],
            dst_ref=rows_in.at[source],
            send_sem=row_send.at[step],
            recv_sem=row_recv.at[source],
            device_id={"sub": peer_sub(step)},
            device_id_type=MESH,
        )

    def build_maps():
        loads[2].wait()
        modes[pl.ds(0, MODES), :] = modes_raw[...]
        mode_rows[own_rows, :] = dot_last(pick[...], modes[...]).astype(BF16)

        def send(step, carry):
            copy_mode(step, front).start()
            return carry

        lax.fori_loop(1, FRONTS, send, 0)

        @pl.when(front > 0)
        def _():
            def one(index, carry):
                rows = tile(index // 4, 1024)
                columns = tile(lax.rem(index, 4), 512)
                product[rows, columns] = dot(inverse[rows, :], coupling[:, columns]).astype(BF16)
                return carry

            lax.fori_loop(0, 8, one, 0)

        @pl.when(high)
        def _():
            turn(product, turned)

        def one(index, carry):
            rows = tile(index, 512)
            modal_map[rows, :] = dot_last(inverse[rows, :], modes[...]).astype(BF16)
            return carry

        lax.fori_loop(0, NF // 512, one, 0)

    def forward(group):
        rows = tile(group, WIDTH)

        @pl.when(front > group * 2)
        def _():
            copy_fwd(group).wait_recv()

            @pl.when(low)
            def _():
                solved_in[group] = dot(solved_in[group], coupling_turned[...]).astype(BF16)

            result = (0.0 - dot(solved_in[group], turned[...])).astype(BF16)
            first = pl.ds(pl.multiple_of(group * WIDTH, WIDTH), OWN)
            second = pl.ds(pl.multiple_of(group * WIDTH + OWN, OWN), OWN)
            solved[first, :] = result[:OWN]

            @pl.when(front > group * 2 + 1)
            def _():
                solved[second, :] = result[OWN:]

        @pl.when(front < FRONTS - 1)
        def _():
            copy_fwd(group).start()

    def backward(group):
        rows = tile(group, WIDTH)

        @pl.when(front < FRONTS - 1)
        def _():
            copy_bwd(group).wait_recv()
            back[rows, :] = (solved[rows, :].astype(F32) - handed_in[group].astype(F32)).astype(BF16)

        @pl.when(front == FRONTS - 1)
        def _():
            back[rows, :] = solved[rows, :]

        @pl.when(front > 0)
        def _():
            handed[group] = dot(back[rows, :], product[...]).astype(BF16)
            copy_bwd(group).start()

        modal_out[group] = dot(back[rows, :], modal_map[...])

        @pl.when(front < FRONTS - 1)
        def _():
            copy_sum(group).wait_recv()
            modal_out[group] = modal_out[group] + modal_in[group]

        @pl.when(front > 0)
        def _():
            copy_sum(group).start()

        @pl.when(front == 0)
        def _():
            modal[rows, :] = modal_out[group].astype(BF16)

            def send(step, carry):
                copy_modal(group, step).start()
                return carry

            lax.fori_loop(1, FRONTS, send, 0)

    map_slot = jnp.where(high, 0, front + 1)

    def slot(moment, carry):
        @pl.when(moment == map_slot)
        def _():
            build_maps()

        ahead = front - moment
        behind = 15 - front - moment

        @pl.when(jnp.logical_and(ahead >= 0, lax.rem(ahead + 16, 2) == 0))
        def _():
            forward(ahead // 2)

        @pl.when(
            jnp.logical_and(
                jnp.logical_and(behind >= 0, behind < 2 * GROUPS), lax.rem(behind + 16, 2) == 0
            )
        )
        def _():
            backward(behind // 2)

        return carry

    lax.fori_loop(0, 16, slot, 0)

    entries[own_rows, :] = dot_last(own[...], back[...])

    def send_entry(step, carry):
        copy_entry(step, front).start()
        return carry

    lax.fori_loop(1, FRONTS, send_entry, 0)

    def displace(index, carry):
        columns = tile(index, 512)
        displaced[:, columns] = dot(back[...], inverse[:, columns])
        return carry

    lax.fori_loop(0, NF // 512, displace, 0)

    @pl.when(front > 0)
    def _():
        def wait(group, carry):
            copy_modal(group, 1).wait_recv()
            return carry

        lax.fori_loop(0, GROUPS, wait, 0)

    def wait_rows(step, carry):
        copy_mode(step, peer_front(step)).wait_recv()
        copy_entry(step, peer_front(step)).wait_recv()
        return carry

    lax.fori_loop(1, FRONTS, wait_rows, 0)
    flexible = (entries[...] - dot_last(mode_rows[...], modal[...])).astype(BF16)
    routed = dot(route[...], flexible).astype(BF16)
    rows_out[...] = routed.reshape(SUBS, SHARE, COLS)

    def send_row(step, carry):
        copy_row(step, sub).start()
        return carry

    lax.fori_loop(1, SUBS, send_row, 0)
    rows_in[sub] = rows_out[sub]

    def deflate(index, carry):
        columns = tile(index, 512)
        attachment[:, columns] = (displaced[:, columns] - dot(modal[...], modes[:, columns])).astype(BF16)
        return carry

    lax.fori_loop(0, NF // 512, deflate, 0)
    store = pltpu.make_async_copy(attachment, attachment_hbm.at[0], store_sem.at[0])
    store.start()

    def wait_row(step, carry):
        copy_row(step, peer_sub(step)).wait_recv()
        return carry

    lax.fori_loop(1, SUBS, wait_row, 0)
    high_place = lax.broadcasted_iota(jnp.int32, (SUBS, SHARE, COLS), 0)

    def spread(index, total):
        level = lax.shift_right_logical(ids_ref[pl.ds(index, 1), :], 7)
        chosen = jnp.where(
            high_place == level[:, None, :], rows_in[index].astype(F32)[None, :, :], 0.0
        ).astype(BF16)
        return total + dot_last(chosen.reshape(SUBS * SHARE, COLS), low_pick[index])

    total = lax.fori_loop(0, SUBS, spread, jnp.zeros((SUBS * SHARE, 128), F32))
    for index in range(SUBS):
        flexibility[:, index * 128 : (index + 1) * 128] = total[index * SHARE : (index + 1) * SHARE]
    store_flexibility = pltpu.make_async_copy(flexibility, flexibility_hbm, store_sem.at[1])
    store_flexibility.start()

    @pl.when(front < FRONTS - 1)
    def _():
        def wait(group, carry):
            copy_fwd(group).wait_send()
            return carry

        lax.fori_loop(0, front // 2 + 1, wait, 0)

    @pl.when(front > 0)
    def _():
        def wait(group, carry):
            copy_bwd(group).wait_send()
            copy_sum(group).wait_send()
            return carry

        lax.fori_loop(0, GROUPS, wait, 0)

    @pl.when(front == 0)
    def _():
        def wait(index, carry):
            copy_modal(index // 7, lax.rem(index, 7) + 1).wait_send()
            return carry

        lax.fori_loop(0, GROUPS * 7, wait, 0)

    def wait_sends(step, carry):
        copy_mode(step, front).wait_send()
        copy_entry(step, front).wait_send()
        return carry

    lax.fori_loop(1, FRONTS, wait_sends, 0)

    def wait_row_sends(step, carry):
        copy_row(step, sub).wait_send()
        return carry

    lax.fori_loop(1, SUBS, wait_row_sends, 0)
    store.wait()
    store_flexibility.wait()


def on_device(front_inverse, coupling, free_modes, dof_offset, interface_id):
    dma = pltpu.SemaphoreType.DMA
    vmem = pltpu.VMEM
    anywhere = pl.BlockSpec(memory_space=pl.ANY)
    local = pl.BlockSpec(memory_space=pltpu.VMEM)
    return pl.pallas_call(
        kernel,
        out_shape=(
            jax.ShapeDtypeStruct((1, COLS, NF), BF16),
            jax.ShapeDtypeStruct((SHARE, NF), F32),
        ),
        in_specs=[anywhere, anywhere, anywhere, local, local],
        out_specs=(anywhere, anywhere),
        scratch_shapes=[
            vmem((NF, NF), BF16),
            vmem((NF, NF), BF16),
            vmem((MODES, NF), BF16),
            vmem((MPAD, NF), BF16),
            vmem((NF, NF), BF16),
            vmem((NF, NF), BF16),
            vmem((NF, NF), BF16),
            vmem((NF, MPAD), BF16),
            vmem((OWN, NF), BF16),
            vmem((OWN, NF), BF16),
            vmem((COLS, NF), BF16),
            vmem((GROUPS, WIDTH, NF), BF16),
            vmem((COLS, NF), BF16),
            vmem((GROUPS, WIDTH, NF), BF16),
            vmem((GROUPS, WIDTH, NF), BF16),
            vmem((GROUPS, WIDTH, MPAD), F32),
            vmem((GROUPS, WIDTH, MPAD), F32),
            vmem((COLS, MPAD), BF16),
            vmem((COLS, MPAD), BF16),
            vmem((COLS, COLS), F32),
            vmem((COLS, COLS), BF16),
            vmem((SUBS, SHARE, COLS), BF16),
            vmem((SUBS, SHARE, COLS), BF16),
            vmem((SUBS, 128, COLS), BF16),
            vmem((COLS, NF), F32),
            vmem((COLS, NF), BF16),
            vmem((SHARE, NF), F32),
            dma((3,)),
            dma((GROUPS,)),
            dma((GROUPS,)),
            dma((GROUPS,)),
            dma((GROUPS,)),
            dma((GROUPS,)),
            dma((GROUPS,)),
            dma((GROUPS, FRONTS)),
            dma((GROUPS,)),
            dma((FRONTS,)),
            dma((FRONTS,)),
            dma((FRONTS,)),
            dma((FRONTS,)),
            dma((SUBS,)),
            dma((SUBS,)),
            dma((2,)),
        ],
        compiler_params=pltpu.CompilerParams(
            collective_id=0, has_side_effects=True, vmem_limit_bytes=60 << 20
        ),
        name="chain",
    )(front_inverse, coupling, free_modes, dof_offset, interface_id)


def solution(mesh):
    return jax.shard_map(
        on_device,
        mesh=mesh,
        in_specs=(
            P("sub", "front", None),
            P("sub", "front", None),
            P("sub", None, "front"),
            P("sub", "front"),
            P(),
        ),
        out_specs=(P("sub", None, "front"), P(("sub", "front"), None)),
        check_vma=False,
    )
```

time: 1090 us -> 119 us (0.11)
  waiting for transfers between devices: 945 us -> 0 us
  Pallas kernels: 0 us -> 114 us
  starting transfers between devices: 67.2 us -> 0 us
  matrix products: 38.6 us -> 0 us
  between operations: 14.1 us -> 0.64 us
  local copies, waits for them, and re-layouts: 15.9 us -> 3.87 us
    reduce_scatter x1 -> x0, waiting for transfers between devices: 657 us -> none  [on_device(): lax.psum_scatter(jnp.dot(selector, spread, precision=lax.Precision.HIGHES...]
    ppermute x16 -> x0, waiting for transfers between devices: 232 us -> none  [shifted(): lax.ppermute(value, axis, [(source, source + steps) for source in range(l...]
    pallas_call x0 -> x1, Pallas kernels: none -> 114 us  [on_device(): pl.pallas_call(kernel, out_shape=(jax.ShapeDtypeStruct((1, COLS, NF), BF1...]
    ppermute x16 -> x0, starting transfers between devices: 66.9 us -> none  [shifted(): lax.ppermute(value, axis, [(source, source + steps) for source in range(l...]
    psum x1 -> x0, waiting for transfers between devices: 56.5 us -> none  [on_device(): lax.psum(contract_last(displacement.astype(jnp.bfloat16), mode_block).ast...]
    dot_general x8 -> x0, matrix products: 38.6 us -> none  [the longest x2 14.1 us: contract_last(): lax.dot_general(left, right, (((1,), (1,)), ((), ())), preferred_element_...]
  transfers between devices with their start and end apart: 18 -> 0, of which waited for: 18 -> 0; matrix products, arithmetic and copies ran while one was open for 0% -> 0% of each run, Pallas kernels for 0% -> 0%
where the time goes in v1:
time: 119 us; the launch traced here: 118 us
  Pallas kernels  114 us (96%)
  local copies, waits for them, and re-layouts  3.87 us (3%)
    pallas_call x1, Pallas kernels, on_device(): pl.pallas_call(kernel, out_shape=(jax.ShapeDtypeStruct((1, COLS, NF), BF1...  114 us
    unnamed x2, local copies, waits for them, and re-layouts  3.87 us

profile of v1, /device:TPU:32, one launch (start us, length us, event | category | flops | bytes accessed | tf_op | source)
XLA Modules:
  0.0 118.1 jit_solution(8328120427810707650)
XLA Ops:
  0.6 113.5 %chain.1 = (bf16[1,256,2048]{2,1,0:T(8,128)(2,1)}, f32[16,2048]{1,0:T(8,128)}) custom-call(bf16[1,2048,2048]{2,1,0:T(8,128)(2,1)} %inverse_hbm.1, bf16[1,2048,2048]{2,1,0:T(8,128)(2,1)} %coupling_hbm.1, bf16[1,300,2048]{2,1,0:T(8,128)(2,1)} %modes_hbm.1, s32[1,32]{1,0:T(1,128)} %offsets_ref.1, s32[16,256]{1,0:T(8,128)} %ids_ref.1), custom_call_target="tpu_custom_call" | custom-call | tf_op jit(solution)/shard_map/chain/pallas_call | solution.py:486
  114.2 2.3 %copy.9 = bf16[1,256,2048]{2,1,0:T(8,128)(2,1)} copy(bf16[1,256,2048]{2,1,0:T(8,128)(2,1)} %get-tuple-element.4) | data formatting | bytes 2097152
  116.5 1.6 %copy.10 = f32[16,2048]{1,0:T(8,128)} copy(f32[16,2048]{1,0:T(8,128)} %get-tuple-element.5) | data formatting | bytes 262144

commit v2 on v1

v2 whole, which is shorter than its diff:
```python
import functools

import jax
import jax.numpy as jnp
from jax import lax
from jax.experimental import pallas as pl
from jax.experimental.pallas import tpu as pltpu
from jax.sharding import PartitionSpec as P

MESH = pl.DeviceIdType.MESH
F32 = jnp.float32
BF16 = jnp.bfloat16

FRONTS = 8
SUBS = 16
NF = 2048
COLS = 256
OWN = 32
GROUPS = 5
WIDTH = 64
VROWS = GROUPS * WIDTH
CHUNK = 512
CHUNKS = NF // CHUNK
MODES = 300
MPAD = 384
SHARE = 16
HIGH = 4
HALF = COLS // 2


def dot(left, right):
    return jnp.dot(left, right, preferred_element_type=F32)


def dot_last(left, right):
    return lax.dot_general(left, right, (((1,), (1,)), ((), ())), preferred_element_type=F32)


def tile(index, size):
    return pl.ds(pl.multiple_of(index * size, size), size)


def kernel(
    inverse_hbm,
    coupling_hbm,
    modes_hbm,
    offsets_ref,
    ids_ref,
    attachment_hbm,
    flexibility_hbm,
    inverse,
    coupling,
    modes_raw,
    modes,
    turned,
    coupling_turned,
    modal_map,
    pick,
    own,
    solved,
    solved_in,
    reduced,
    back,
    handed,
    handed_in,
    modal_out,
    modal_in,
    modal,
    mode_rows,
    entries,
    route,
    rows_out,
    rows_in,
    low_pick,
    displaced,
    attachment,
    flexibility,
    inverse_sem,
    coupling_sem,
    modes_sem,
    fwd_send,
    fwd_recv,
    bwd_send,
    bwd_recv,
    sum_send,
    sum_recv,
    modal_send,
    modal_recv,
    mode_send,
    mode_recv,
    entry_send,
    entry_recv,
    row_send,
    row_recv,
    store_sem,
):
    front = lax.axis_index("front")
    sub = lax.axis_index("sub")
    subs = lax.axis_size("sub")
    last = FRONTS - 1
    high = front >= HIGH
    low = front < HIGH

    def chunk(index):
        return tile(index, CHUNK)

    def load_inverse(index):
        rows = chunk(index)
        return pltpu.make_async_copy(inverse_hbm.at[0, rows], inverse.at[rows], inverse_sem.at[index])

    def load_coupling(index):
        rows = chunk(index)
        return pltpu.make_async_copy(coupling_hbm.at[0, rows], coupling.at[rows], coupling_sem.at[index])

    load_modes = pltpu.make_async_copy(modes_hbm.at[0], modes_raw, modes_sem)
    for index in range(CHUNKS):
        load_inverse(index).start()
    for index in range(CHUNKS):
        load_coupling(index).start()
    load_modes.start()

    def peer_front(step):
        return lax.rem(front + step, FRONTS)

    def peer_sub(step):
        return lax.rem(sub + step, subs)

    barrier = pltpu.get_barrier_semaphore()

    def greet_front(step, carry):
        pl.semaphore_signal(barrier, inc=1, device_id={"front": peer_front(step)}, device_id_type=MESH)
        return carry

    def greet_sub(step, carry):
        pl.semaphore_signal(barrier, inc=1, device_id={"sub": peer_sub(step)}, device_id_type=MESH)
        return carry

    lax.fori_loop(1, FRONTS, greet_front, 0)
    lax.fori_loop(1, subs, greet_sub, 0)

    offsets_square = jnp.broadcast_to(offsets_ref[...].astype(F32), (OWN, OWN))
    diagonal = lax.broadcasted_iota(jnp.int32, (OWN, OWN), 0) == lax.broadcasted_iota(
        jnp.int32, (OWN, OWN), 1
    )
    offsets_column = jnp.sum(
        jnp.where(diagonal, offsets_square, 0.0), axis=1, keepdims=True
    ).astype(jnp.int32)
    pick[...] = (offsets_column == lax.broadcasted_iota(jnp.int32, (OWN, NF), 1)).astype(F32).astype(BF16)
    solved[...] = jnp.zeros((VROWS, NF), BF16)
    solved_in[0, :OWN] = jnp.zeros((OWN, NF), BF16)
    handed_in[0, :OWN] = jnp.zeros((OWN, NF), BF16)
    modal_in[0, :OWN] = jnp.zeros((OWN, MPAD), F32)

    @pl.when(front == 0)
    def _():
        def one(index, carry):
            load_inverse(index).wait()
            own[:, chunk(index)] = dot_last(pick[...], inverse[chunk(index), :]).astype(BF16)
            return carry

        lax.fori_loop(0, CHUNKS, one, 0)

    @pl.when(front > 0)
    def _():
        def one(index, carry):
            load_inverse(index).wait()
            block = inverse[chunk(index), :].T
            turned[:, chunk(index)] = block
            own[:, chunk(index)] = dot(pick[...], block).astype(BF16)
            return carry

        lax.fori_loop(0, CHUNKS, one, 0)

    own_virtual = pl.ds(pl.multiple_of(front * OWN + OWN, OWN), OWN)
    solved[own_virtual, :] = own[...]
    pl.semaphore_wait(barrier, FRONTS - 1 + subs - 1)

    def rows_of(group):
        return tile(group, WIDTH)

    def second_of(group):
        return pl.ds(pl.multiple_of(group * WIDTH + OWN, OWN), OWN)

    after = jnp.minimum(front + 1, last)
    before = jnp.maximum(front - 1, 0)
    whole = pl.ds(0, NF)

    def copy_fwd(group, small, columns):
        inner = pl.ds(OWN, OWN) if small else pl.ds(0, WIDTH)
        return pltpu.make_async_remote_copy(
            src_ref=solved.at[second_of(group) if small else rows_of(group), columns],
            dst_ref=solved_in.at[group, inner, columns],
            send_sem=fwd_send.at[group],
            recv_sem=fwd_recv.at[group],
            device_id={"front": after},
            device_id_type=MESH,
        )

    def copy_bwd(group, small, columns):
        inner = pl.ds(OWN, OWN) if small else pl.ds(0, WIDTH)
        return pltpu.make_async_remote_copy(
            src_ref=handed.at[group, inner, columns],
            dst_ref=handed_in.at[group, inner, columns],
            send_sem=bwd_send.at[group],
            recv_sem=bwd_recv.at[group],
            device_id={"front": before},
            device_id_type=MESH,
        )

    def copy_sum(group, small):
        inner = pl.ds(OWN, OWN) if small else pl.ds(0, WIDTH)
        return pltpu.make_async_remote_copy(
            src_ref=modal_out.at[group, inner],
            dst_ref=modal_in.at[group, inner],
            send_sem=sum_send.at[group],
            recv_sem=sum_recv.at[group],
            device_id={"front": before},
            device_id_type=MESH,
        )

    def copy_modal(group, small, step):
        rows = second_of(group) if small else rows_of(group)
        return pltpu.make_async_remote_copy(
            src_ref=modal.at[rows],
            dst_ref=modal.at[rows],
            send_sem=modal_send.at[group, step],
            recv_sem=modal_recv.at[group],
            device_id={"front": peer_front(step)},
            device_id_type=MESH,
        )

    def by_size(group, act):
        @pl.when(group == 0)
        def _():
            act(True)

        @pl.when(group > 0)
        def _():
            act(False)

    def own_part(index):
        return pl.ds(pl.multiple_of(index * OWN, OWN), OWN)

    def copy_mode(step, index):
        rows = own_part(index)
        return pltpu.make_async_remote_copy(
            src_ref=mode_rows.at[rows],
            dst_ref=mode_rows.at[rows],
            send_sem=mode_send.at[step],
            recv_sem=mode_recv.at[index],
            device_id={"front": peer_front(step)},
            device_id_type=MESH,
        )

    def copy_entry(half, step, index):
        rows = own_part(index)
        return pltpu.make_async_remote_copy(
            src_ref=entries.at[half, rows],
            dst_ref=entries.at[half, rows],
            send_sem=entry_send.at[half, step],
            recv_sem=entry_recv.at[half, index],
            device_id={"front": peer_front(step)},
            device_id_type=MESH,
        )

    def copy_row(step, source):
        return pltpu.make_async_remote_copy(
            src_ref=rows_out.at[peer_sub(step)],
            dst_ref=rows_in.at[source],
            send_sem=row_send.at[step],
            recv_sem=row_recv.at[source],
            device_id={"sub": peer_sub(step)},
            device_id_type=MESH,
        )

    @pl.when(front == 0)
    def _():
        copy_fwd(0, True, whole).start()

    @pl.when(front > 0)
    def _():
        def one(index, carry):
            load_coupling(index).wait()
            coupling_turned[:, chunk(index)] = coupling[chunk(index), :].T
            return carry

        lax.fori_loop(0, CHUNKS, one, 0)

    @pl.when(front == 0)
    def _():
        def one(index, carry):
            load_coupling(index).wait()
            return carry

        lax.fori_loop(0, CHUNKS, one, 0)

    def build_maps():
        load_modes.wait()
        modes[...] = jnp.zeros((MPAD, NF), BF16)
        modes[pl.ds(0, MODES), :] = modes_raw[...]
        mode_rows[own_part(front), :] = dot_last(pick[...], modes[...]).astype(BF16)

        def send(step, carry):
            copy_mode(step, front).start()
            return carry

        lax.fori_loop(1, FRONTS, send, 0)

        place = lax.broadcasted_iota(jnp.int32, (COLS, COLS), 0)
        target = (
            lax.shift_right_logical(place, 4) * (FRONTS * SHARE)
            + jnp.bitwise_and(place, 15)
            + front * SHARE
        )
        route[...] = (target == ids_ref[pl.ds(sub, 1), :]).astype(F32).astype(BF16)
        lane_place = lax.broadcasted_iota(jnp.int32, (128, COLS), 0)

        def fill_low(index, carry):
            ids = jnp.bitwise_and(ids_ref[pl.ds(index, 1), :], 127)
            low_pick[index] = (lane_place == ids).astype(F32).astype(BF16)
            return carry

        lax.fori_loop(0, SUBS, fill_low, 0)

        @pl.when(jnp.logical_and(low, front > 0))
        def _():
            def one(index, carry):
                rows = tile(index // 4, 1024)
                columns = chunk(lax.rem(index, 4))
                turned[rows, columns] = dot(inverse[rows, :], coupling[:, columns]).astype(BF16)
                return carry

            lax.fori_loop(0, 8, one, 0)

        @pl.when(low)
        def _():
            def one(index, carry):
                rows = chunk(index)
                modal_map[rows, :] = dot_last(inverse[rows, :], modes[...]).astype(BF16)
                return carry

            lax.fori_loop(0, CHUNKS, one, 0)

    def forward(group):
        arrives = front >= jnp.maximum(2 * group, 1)

        @pl.when(arrives)
        def _():
            by_size(group, lambda small: copy_fwd(group, small, whole).wait_recv())
            reduced[...] = dot(solved_in[group], coupling_turned[...]).astype(BF16)
            for index in range(CHUNKS):
                columns = pl.ds(index * CHUNK, CHUNK)
                result = (0.0 - dot(reduced[...], turned[:, columns])).astype(BF16)
                solved[tile(group * 2, OWN), columns] = result[:OWN]

                @pl.when(front > group * 2)
                def _():
                    solved[second_of(group), columns] = result[OWN:]

                @pl.when(front < last)
                def _():
                    by_size(group, lambda small: copy_fwd(group, small, columns).start())

        @pl.when(jnp.logical_and(front < last, front == 2 * group - 1))
        def _():
            copy_fwd(group, False, whole).start()

    def send_entries(half):
        columns = pl.ds(OWN + half * HALF, HALF)
        entries[half, own_part(front)] = dot_last(own[...], back[columns, :])
        for step in (4, 5, 3, 2, 6, 7, 1):
            copy_entry(half, step, front).start()

    def backward(group):
        rows = rows_of(group)

        @pl.when(front < last)
        def _():
            by_size(group, lambda small: copy_bwd(group, small, whole).wait_recv())
            back[rows, :] = (solved[rows, :].astype(F32) - handed_in[group].astype(F32)).astype(BF16)

        @pl.when(front == last)
        def _():
            back[rows, :] = solved[rows, :]

        @pl.when(low)
        def _():
            @pl.when(front > 0)
            def _():
                for index in range(CHUNKS):
                    columns = pl.ds(index * CHUNK, CHUNK)
                    handed[group, :, columns] = dot(back[rows, :], turned[:, columns]).astype(BF16)
                    by_size(group, lambda small: copy_bwd(group, small, columns).start())

            modal_out[group] = dot(back[rows, :], modal_map[...])

        @pl.when(high)
        def _():
            moved = dot(back[rows, :], inverse[...])
            displaced[rows, :] = moved
            reduced[...] = moved.astype(BF16)
            for index in range(CHUNKS):
                columns = pl.ds(index * CHUNK, CHUNK)
                handed[group, :, columns] = dot(reduced[...], coupling[:, columns]).astype(BF16)
                by_size(group, lambda small: copy_bwd(group, small, columns).start())
            modal_out[group] = dot_last(reduced[...], modes[...])

        @pl.when(front < last)
        def _():
            by_size(group, lambda small: copy_sum(group, small).wait_recv())
            modal_out[group] = modal_out[group] + modal_in[group]

        @pl.when(front > 0)
        def _():
            by_size(group, lambda small: copy_sum(group, small).start())

        @pl.when(front == 0)
        def _():
            modal[rows, :] = modal_out[group].astype(BF16)

            def send(small):
                for step in (4, 5, 3, 2, 6, 7, 1):
                    copy_modal(group, small, step).start()

            by_size(group, send)

        @pl.when(group == 1)
        def _():
            send_entries(1)

    map_slot = jnp.where(high, 0, front + 2)

    def slot(moment, carry):
        @pl.when(moment == map_slot)
        def _():
            build_maps()

        ahead = front + 1 - moment
        behind = 16 - front - moment

        @pl.when(jnp.logical_and(ahead >= 0, lax.rem(ahead + 16, 2) == 0))
        def _():
            forward(ahead // 2)

        @pl.when(
            jnp.logical_and(
                jnp.logical_and(behind >= 0, behind < 2 * GROUPS), lax.rem(behind + 16, 2) == 0
            )
        )
        def _():
            backward(behind // 2)

        return carry

    lax.fori_loop(0, 17, slot, 0)
    send_entries(0)
    real = pl.ds(OWN, COLS)

    @pl.when(low)
    def _():
        def displace(index, carry):
            columns = chunk(index)
            displaced[real, columns] = dot(back[real, :], inverse[:, columns])
            return carry

        lax.fori_loop(0, CHUNKS, displace, 0)

    @pl.when(front > 0)
    def _():
        def wait(group, carry):
            copy_modal(group, False, 1).wait_recv()
            return carry

        lax.fori_loop(1, GROUPS, wait, 0)
        copy_modal(0, True, 1).wait_recv()

    def wait_rows(step, carry):
        copy_mode(step, peer_front(step)).wait_recv()
        copy_entry(0, step, peer_front(step)).wait_recv()
        copy_entry(1, step, peer_front(step)).wait_recv()
        return carry

    lax.fori_loop(1, FRONTS, wait_rows, 0)
    projected = dot_last(mode_rows[...], modal[real, :])
    for half in range(2):
        lanes = slice(half * HALF, (half + 1) * HALF)
        flexible = (entries[half] - projected[:, lanes]).astype(BF16)
        rows_out[:, :, lanes] = dot(route[...], flexible).astype(BF16).reshape(SUBS, SHARE, HALF)

    def send_row(step, carry):
        copy_row(step, sub).start()
        return carry

    lax.fori_loop(1, subs, send_row, 0)
    rows_in[sub] = rows_out[sub]

    def deflate(index, carry):
        columns = chunk(index)
        attachment[:, columns] = (
            displaced[real, columns] - dot(modal[real, :], modes[:, columns])
        ).astype(BF16)
        return carry

    lax.fori_loop(0, CHUNKS, deflate, 0)
    store = pltpu.make_async_copy(attachment, attachment_hbm.at[0], store_sem.at[0])
    store.start()

    def wait_row(step, carry):
        copy_row(step, peer_sub(step)).wait_recv()
        return carry

    lax.fori_loop(1, subs, wait_row, 0)
    high_place = lax.broadcasted_iota(jnp.int32, (SUBS, SHARE, COLS), 0)

    def spread(index, total):
        level = lax.shift_right_logical(ids_ref[pl.ds(index, 1), :], 7)
        chosen = jnp.where(
            high_place == level[:, None, :], rows_in[index].astype(F32)[None, :, :], 0.0
        ).astype(BF16)
        return total + dot_last(chosen.reshape(SUBS * SHARE, COLS), low_pick[index])

    total = lax.fori_loop(0, SUBS, spread, jnp.zeros((SUBS * SHARE, 128), F32))
    for index in range(SUBS):
        flexibility[:, index * 128 : (index + 1) * 128] = total[index * SHARE : (index + 1) * SHARE]
    store_flexibility = pltpu.make_async_copy(flexibility, flexibility_hbm, store_sem.at[1])
    store_flexibility.start()

    @pl.when(front < last)
    def _():
        copy_fwd(0, True, whole).wait_send()

        def wait(group, carry):
            copy_fwd(group, False, whole).wait_send()
            return carry

        lax.fori_loop(1, (front + 1) // 2 + 1, wait, 0)

    @pl.when(front > 0)
    def _():
        copy_bwd(0, True, whole).wait_send()
        copy_sum(0, True).wait_send()

        def wait(group, carry):
            copy_bwd(group, False, whole).wait_send()
            copy_sum(group, False).wait_send()
            return carry

        lax.fori_loop(1, GROUPS, wait, 0)

    @pl.when(front == 0)
    def _():
        def wait(index, carry):
            copy_modal(index // 7, False, lax.rem(index, 7) + 1).wait_send()
            return carry

        lax.fori_loop(7, GROUPS * 7, wait, 0)

        def wait_small(index, carry):
            copy_modal(0, True, index).wait_send()
            return carry

        lax.fori_loop(1, FRONTS, wait_small, 0)

    def wait_sends(step, carry):
        copy_mode(step, front).wait_send()
        copy_entry(0, step, front).wait_send()
        copy_entry(1, step, front).wait_send()
        return carry

    lax.fori_loop(1, FRONTS, wait_sends, 0)

    def wait_row_sends(step, carry):
        copy_row(step, sub).wait_send()
        return carry

    lax.fori_loop(1, subs, wait_row_sends, 0)
    store.wait()
    store_flexibility.wait()


def on_device(front_inverse, coupling, free_modes, dof_offset, interface_id):
    dma = pltpu.SemaphoreType.DMA
    vmem = pltpu.VMEM
    anywhere = pl.BlockSpec(memory_space=pl.ANY)
    local = pl.BlockSpec(memory_space=pltpu.VMEM)
    return pl.pallas_call(
        kernel,
        out_shape=(
            jax.ShapeDtypeStruct((1, COLS, NF), BF16),
            jax.ShapeDtypeStruct((SHARE, NF), F32),
        ),
        in_specs=[anywhere, anywhere, anywhere, local, local],
        out_specs=(anywhere, anywhere),
        scratch_shapes=[
            vmem((NF, NF), BF16),
            vmem((NF, NF), BF16),
            vmem((MODES, NF), BF16),
            vmem((MPAD, NF), BF16),
            vmem((NF, NF), BF16),
            vmem((NF, NF), BF16),
            vmem((NF, MPAD), BF16),
            vmem((OWN, NF), BF16),
            vmem((OWN, NF), BF16),
            vmem((VROWS, NF), BF16),
            vmem((GROUPS, WIDTH, NF), BF16),
            vmem((WIDTH, NF), BF16),
            vmem((VROWS, NF), BF16),
            vmem((GROUPS, WIDTH, NF), BF16),
            vmem((GROUPS, WIDTH, NF), BF16),
            vmem((GROUPS, WIDTH, MPAD), F32),
            vmem((GROUPS, WIDTH, MPAD), F32),
            vmem((VROWS, MPAD), BF16),
            vmem((COLS, MPAD), BF16),
            vmem((2, COLS, HALF), F32),
            vmem((COLS, COLS), BF16),
            vmem((SUBS, SHARE, COLS), BF16),
            vmem((SUBS, SHARE, COLS), BF16),
            vmem((SUBS, 128, COLS), BF16),
            vmem((VROWS, NF), F32),
            vmem((COLS, NF), BF16),
            vmem((SHARE, NF), F32),
            dma((CHUNKS,)),
            dma((CHUNKS,)),
            dma,
            dma((GROUPS,)),
            dma((GROUPS,)),
            dma((GROUPS,)),
            dma((GROUPS,)),
            dma((GROUPS,)),
            dma((GROUPS,)),
            dma((GROUPS, FRONTS)),
            dma((GROUPS,)),
            dma((FRONTS,)),
            dma((FRONTS,)),
            dma((2, FRONTS)),
            dma((2, FRONTS)),
            dma((SUBS,)),
            dma((SUBS,)),
            dma((2,)),
        ],
        compiler_params=pltpu.CompilerParams(
            collective_id=0, has_side_effects=True, vmem_limit_bytes=60 << 20
        ),
        name="chain",
    )(front_inverse, coupling, free_modes, dof_offset, interface_id)


def solution(mesh):
    return jax.shard_map(
        on_device,
        mesh=mesh,
        in_specs=(
            P("sub", "front", None),
            P("sub", "front", None),
            P("sub", None, "front"),
            P("sub", "front"),
            P(),
        ),
        out_specs=(P("sub", None, "front"), P(("sub", "front"), None)),
        check_vma=False,
    )
```

time: 119 us -> 109 us (0.916)
  Pallas kernels: 114 us -> 104 us
    pallas_call x1, Pallas kernels: 114 us -> 104 us  [on_device(): pl.pallas_call(kernel, out_shape=(jax.ShapeDtypeStruct((1, COLS, NF), BF1...]
where the time goes in v2:
time: 109 us
  Pallas kernels  104 us (95%)
  local copies, waits for them, and re-layouts  3.87 us (4%)
    pallas_call x1, Pallas kernels, on_device(): pl.pallas_call(kernel, out_shape=(jax.ShapeDtypeStruct((1, COLS, NF), BF1...  104 us
    unnamed x2, local copies, waits for them, and re-layouts  3.87 us

profile of v2, /device:TPU:32, one launch (start us, length us, event | category | flops | bytes accessed | tf_op | source)
XLA Modules:
  0.0 108.7 jit_solution(16026163142855112180)
XLA Ops:
  0.6 104.1 %chain.1 = (bf16[1,256,2048]{2,1,0:T(8,128)(2,1)}, f32[16,2048]{1,0:T(8,128)}) custom-call(bf16[1,2048,2048]{2,1,0:T(8,128)(2,1)} %inverse_hbm.1, bf16[1,2048,2048]{2,1,0:T(8,128)(2,1)} %coupling_hbm.1, bf16[1,300,2048]{2,1,0:T(8,128)(2,1)} %modes_hbm.1, s32[1,32]{1,0:T(1,128)} %offsets_ref.1, s32[16,256]{1,0:T(8,128)} %ids_ref.1), custom_call_target="tpu_custom_call" | custom-call | tf_op jit(solution)/shard_map/chain/pallas_call | solution.py:586
  104.8 2.3 %copy.9 = bf16[1,256,2048]{2,1,0:T(8,128)(2,1)} copy(bf16[1,256,2048]{2,1,0:T(8,128)(2,1)} %get-tuple-element.4) | data formatting | bytes 2097152
  107.1 1.6 %copy.10 = f32[16,2048]{1,0:T(8,128)} copy(f32[16,2048]{1,0:T(8,128)} %get-tuple-element.5) | data formatting | bytes 262144

commit v3 on v2

v3 whole, which is shorter than its diff:
```python
import functools

import jax
import jax.numpy as jnp
from jax import lax
from jax.experimental import pallas as pl
from jax.experimental.pallas import tpu as pltpu
from jax.sharding import PartitionSpec as P

MESH = pl.DeviceIdType.MESH
F32 = jnp.float32
BF16 = jnp.bfloat16

FRONTS = 8
SUBS = 16
NF = 2048
COLS = 256
OWN = 32
STARTS = (0, 1, 3, 5, 8)
GROUPS = len(STARTS) - 1
CHUNK = 512
CHUNKS = NF // CHUNK
MODES = 300
MPAD = 384
SHARE = 16
HALF = COLS // 2


def dot(left, right):
    return jnp.dot(left, right, preferred_element_type=F32)


def dot_last(left, right):
    return lax.dot_general(left, right, (((1,), (1,)), ((), ())), preferred_element_type=F32)


def dot_wide(left, right):
    count = left.shape[0]
    if count < 128:
        left = jnp.concatenate([left, left, left, left][: 128 // count] + [left[: 128 % count]] * (128 % count > 0), axis=0)
    return dot(left, right)[:count]


def tile(index, size):
    return pl.ds(pl.multiple_of(index * size, size), size)


def kernel(
    inverse_hbm,
    coupling_hbm,
    modes_hbm,
    offsets_ref,
    ids_ref,
    attachment_hbm,
    flexibility_hbm,
    inverse,
    coupling,
    modes_raw,
    modes,
    turned,
    coupling_turned,
    modal_map,
    gathered,
    pick,
    own,
    solved,
    solved_in,
    reduced,
    back,
    handed,
    handed_in,
    modal_out,
    modal_in,
    modal,
    mode_rows,
    entries,
    route,
    rows_out,
    rows_in,
    low_pick,
    displaced,
    attachment,
    flexibility,
    inverse_sem,
    coupling_sem,
    modes_sem,
    fwd_send,
    fwd_recv,
    bwd_send,
    bwd_recv,
    sum_send,
    sum_recv,
    modal_send,
    modal_recv,
    mode_send,
    mode_recv,
    entry_send,
    entry_recv,
    row_send,
    row_recv,
    store_sem,
):
    front = lax.axis_index("front")
    sub = lax.axis_index("sub")
    subs = lax.axis_size("sub")
    last = FRONTS - 1

    def chunk(index):
        return tile(index, CHUNK)

    def load_inverse(index):
        rows = chunk(index)
        return pltpu.make_async_copy(inverse_hbm.at[0, rows], inverse.at[rows], inverse_sem.at[index])

    def load_coupling(index):
        rows = chunk(index)
        return pltpu.make_async_copy(coupling_hbm.at[0, rows], coupling.at[rows], coupling_sem.at[index])

    load_modes = pltpu.make_async_copy(modes_hbm.at[0], modes_raw, modes_sem)
    for index in range(CHUNKS):
        load_inverse(index).start()
    for index in range(CHUNKS):
        load_coupling(index).start()
    load_modes.start()

    def peer_front(step):
        return lax.rem(front + step, FRONTS)

    def peer_sub(step):
        return lax.rem(sub + step, subs)

    barrier = pltpu.get_barrier_semaphore()

    def greet_front(step, carry):
        pl.semaphore_signal(barrier, inc=1, device_id={"front": peer_front(step)}, device_id_type=MESH)
        return carry

    def greet_sub(step, carry):
        pl.semaphore_signal(barrier, inc=1, device_id={"sub": peer_sub(step)}, device_id_type=MESH)
        return carry

    lax.fori_loop(1, FRONTS, greet_front, 0)
    lax.fori_loop(1, subs, greet_sub, 0)

    offsets_square = jnp.broadcast_to(offsets_ref[...].astype(F32), (OWN, OWN))
    diagonal = lax.broadcasted_iota(jnp.int32, (OWN, OWN), 0) == lax.broadcasted_iota(
        jnp.int32, (OWN, OWN), 1
    )
    offsets_column = jnp.sum(
        jnp.where(diagonal, offsets_square, 0.0), axis=1, keepdims=True
    ).astype(jnp.int32)
    pick[...] = (offsets_column == lax.broadcasted_iota(jnp.int32, (OWN, NF), 1)).astype(F32).astype(BF16)
    solved[...] = jnp.zeros((COLS, NF), BF16)

    @pl.when(front == 0)
    def _():
        def one(index, carry):
            load_inverse(index).wait()
            own[:, chunk(index)] = dot_last(pick[...], inverse[chunk(index), :]).astype(BF16)
            return carry

        lax.fori_loop(0, CHUNKS, one, 0)

    @pl.when(front > 0)
    def _():
        def one(index, carry):
            load_inverse(index).wait()
            block = inverse[chunk(index), :].T
            turned[:, chunk(index)] = block
            own[:, chunk(index)] = dot(pick[...], block).astype(BF16)
            return carry

        lax.fori_loop(0, CHUNKS, one, 0)

    own_rows = pl.ds(pl.multiple_of(front * OWN, OWN), OWN)
    solved[own_rows, :] = own[...]
    pl.semaphore_wait(barrier, FRONTS - 1 + subs - 1)

    def rows_of(group):
        return slice(STARTS[group] * OWN, STARTS[group + 1] * OWN)

    def count_of(group):
        return (STARTS[group + 1] - STARTS[group]) * OWN

    after = jnp.minimum(front + 1, last)
    before = jnp.maximum(front - 1, 0)
    whole = slice(0, NF)

    def chunk_lanes(index):
        return slice(index * CHUNK, (index + 1) * CHUNK)

    def copy_fwd(group, index, columns=None):
        columns = chunk_lanes(index) if columns is None else columns
        return pltpu.make_async_remote_copy(
            src_ref=solved.at[rows_of(group), columns],
            dst_ref=solved_in.at[rows_of(group), columns],
            send_sem=fwd_send.at[group],
            recv_sem=fwd_recv.at[group, index],
            device_id={"front": after},
            device_id_type=MESH,
        )

    def copy_bwd(group, index, columns=None):
        columns = chunk_lanes(index) if columns is None else columns
        return pltpu.make_async_remote_copy(
            src_ref=handed.at[rows_of(group), columns],
            dst_ref=handed_in.at[rows_of(group), columns],
            send_sem=bwd_send.at[group],
            recv_sem=bwd_recv.at[group, index],
            device_id={"front": before},
            device_id_type=MESH,
        )

    def copy_sum(group):
        return pltpu.make_async_remote_copy(
            src_ref=modal_out.at[rows_of(group)],
            dst_ref=modal_in.at[rows_of(group)],
            send_sem=sum_send.at[group],
            recv_sem=sum_recv.at[group],
            device_id={"front": before},
            device_id_type=MESH,
        )

    def copy_modal(group, step):
        return pltpu.make_async_remote_copy(
            src_ref=modal.at[rows_of(group)],
            dst_ref=modal.at[rows_of(group)],
            send_sem=modal_send.at[group, step],
            recv_sem=modal_recv.at[group],
            device_id={"front": peer_front(step)},
            device_id_type=MESH,
        )

    def own_part(index):
        return pl.ds(pl.multiple_of(index * OWN, OWN), OWN)

    def copy_mode(step, index):
        rows = own_part(index)
        return pltpu.make_async_remote_copy(
            src_ref=mode_rows.at[rows],
            dst_ref=mode_rows.at[rows],
            send_sem=mode_send.at[step],
            recv_sem=mode_recv.at[index],
            device_id={"front": peer_front(step)},
            device_id_type=MESH,
        )

    def copy_entry(half, step, index):
        rows = own_part(index)
        return pltpu.make_async_remote_copy(
            src_ref=entries.at[half, rows],
            dst_ref=entries.at[half, rows],
            send_sem=entry_send.at[half, step],
            recv_sem=entry_recv.at[half, index],
            device_id={"front": peer_front(step)},
            device_id_type=MESH,
        )

    def copy_row(step, source):
        return pltpu.make_async_remote_copy(
            src_ref=rows_out.at[peer_sub(step)],
            dst_ref=rows_in.at[source],
            send_sem=row_send.at[step],
            recv_sem=row_recv.at[source],
            device_id={"sub": peer_sub(step)},
            device_id_type=MESH,
        )

    @pl.when(front == 0)
    def _():
        for index in range(CHUNKS):
            copy_fwd(0, index).start()

    @pl.when(front > 1)
    def _():
        def one(index, carry):
            load_coupling(index).wait()
            coupling_turned[:, chunk(index)] = coupling[chunk(index), :].T
            return carry

        lax.fori_loop(0, CHUNKS, one, 0)

    @pl.when(front <= 1)
    def _():
        def one(index, carry):
            load_coupling(index).wait()
            return carry

        lax.fori_loop(0, CHUNKS, one, 0)

    def build_modal_map():
        load_modes.wait()
        modes[...] = jnp.zeros((MPAD, NF), BF16)
        modes[pl.ds(0, MODES), :] = modes_raw[...]

        @pl.when(front == 0)
        def _():
            def one(index, carry):
                rows = chunk(index)
                modal_map[rows, :] = dot_last(inverse[rows, :], modes[...]).astype(BF16)
                return carry

            lax.fori_loop(0, CHUNKS, one, 0)

        @pl.when(front > 0)
        def _():
            def one(index, carry):
                rows = chunk(index)
                modal_map[rows, :] = modes[:, rows].T
                return carry

            lax.fori_loop(0, CHUNKS, one, 0)

    def build_picks():
        mode_rows[own_part(front), :] = dot_last(pick[...], modes[...]).astype(BF16)

        def send(step, carry):
            copy_mode(step, front).start()
            return carry

        lax.fori_loop(1, FRONTS, send, 0)

        place = lax.broadcasted_iota(jnp.int32, (COLS, COLS), 0)
        target = (
            lax.shift_right_logical(place, 4) * (FRONTS * SHARE)
            + jnp.bitwise_and(place, 15)
            + front * SHARE
        )
        route[...] = (target == ids_ref[pl.ds(sub, 1), :]).astype(F32).astype(BF16)
        lane_place = lax.broadcasted_iota(jnp.int32, (128, COLS), 0)

        def fill_low(index, carry):
            ids = jnp.bitwise_and(ids_ref[pl.ds(index, 1), :], 127)
            low_pick[index] = (lane_place == ids).astype(F32).astype(BF16)
            return carry

        lax.fori_loop(0, SUBS, fill_low, 0)

    def forward(group):
        rows = rows_of(group)
        count = count_of(group)
        first = STARTS[group]
        members = STARTS[group + 1] - first

        if group == 0:

            @pl.when(front == 1)
            def _():
                for index in range(CHUNKS):
                    columns = chunk_lanes(index)
                    copy_fwd(group, index).wait_recv()
                    part = dot_last(solved_in[rows, columns], coupling[:, columns])
                    gathered[:count] = part if index == 0 else gathered[:count] + part
                reduced[:count] = gathered[:count].astype(BF16)

        @pl.when(front > max(first, 1))
        def _():
            for index in range(CHUNKS):
                columns = chunk_lanes(index)
                copy_fwd(group, index).wait_recv()
                part = dot_wide(solved_in[rows, columns], coupling_turned[columns, :])
                if index == 0:
                    gathered[:count] = part
                elif index < CHUNKS - 1:
                    gathered[:count] = gathered[:count] + part
                else:
                    reduced[:count] = (gathered[:count] + part).astype(BF16)

        @pl.when(front > first)
        def _():
            for index in range(CHUNKS):
                columns = chunk_lanes(index)
                result = (0.0 - dot_wide(reduced[:count], turned[:, columns])).astype(BF16)
                solved[first * OWN : (first + 1) * OWN, columns] = result[:OWN]
                for member in range(1, members):

                    @pl.when(front > first + member)
                    def _():
                        part = slice(member * OWN, (member + 1) * OWN)
                        solved[(first + member) * OWN : (first + member + 1) * OWN, columns] = result[part]

                @pl.when(front < last)
                def _():
                    copy_fwd(group, index).start()

        if group > 0:

            @pl.when(front == first)
            def _():
                for index in range(CHUNKS):
                    copy_fwd(group, index).start()

    def send_entries(half):
        columns = pl.ds(half * HALF, HALF)
        entries[half, own_part(front)] = dot_last(own[...], back[columns, :])
        for step in (4, 5, 3, 2, 6, 7, 1):
            copy_entry(half, step, front).start()

    def backward(group):
        rows = rows_of(group)
        count = count_of(group)
        for index in range(CHUNKS):
            columns = chunk_lanes(index)

            @pl.when(front < last)
            def _():
                copy_bwd(group, index).wait_recv()
                back[rows, columns] = (
                    solved[rows, columns].astype(F32) - handed_in[rows, columns].astype(F32)
                ).astype(BF16)

            @pl.when(front == last)
            def _():
                back[rows, columns] = solved[rows, columns]

            @pl.when(front > 0)
            def _():
                total = dot_wide(back[rows, columns], inverse[columns, :])
                if index > 0:
                    total = displaced[rows, :] + total
                displaced[rows, :] = total
                if index == CHUNKS - 1:
                    reduced[:count] = total.astype(BF16)

            @pl.when(front == 0)
            def _():
                part = dot_wide(back[rows, columns], modal_map[columns, :])
                modal_out[rows, :] = part if index == 0 else modal_out[rows, :] + part

        @pl.when(front > 0)
        def _():
            for index in range(CHUNKS):
                columns = chunk_lanes(index)
                handed[rows, columns] = dot_wide(reduced[:count], coupling[:, columns]).astype(BF16)
                copy_bwd(group, index).start()

            modal_out[rows, :] = dot_wide(reduced[:count], modal_map[...])

        @pl.when(front < last)
        def _():
            copy_sum(group).wait_recv()
            modal_out[rows, :] = modal_out[rows, :] + modal_in[rows, :]

        @pl.when(front > 0)
        def _():
            copy_sum(group).start()

        @pl.when(front == 0)
        def _():
            modal[rows, :] = modal_out[rows, :].astype(BF16)
            for step in (4, 5, 3, 2, 6, 7, 1):
                copy_modal(group, step).start()
            if group > 0:
                displaced[rows, :] = dot_wide(back[rows, :], inverse[...])

        if group == 2:
            send_entries(1)

    build_modal_at = jnp.where(front < 2, 5, 0)
    build_picks_at = jnp.where(front < 4, 9, 99)

    def slot(moment, carry):
        @pl.when(moment == build_modal_at)
        def _():
            build_modal_map()

        @pl.when(moment == build_picks_at)
        def _():
            build_picks()

        for group in range(GROUPS):
            turn_f = 2 * (front - STARTS[group])
            turn_b = 2 * (15 - STARTS[group] - front) + jnp.where(front >= last - 1, -1, 1)

            @pl.when(moment == turn_f)
            def _():
                forward(group)

            @pl.when(moment == turn_b)
            def _():
                backward(group)

        return carry

    lax.fori_loop(0, 32, slot, 0)
    send_entries(0)

    @pl.when(front >= 4)
    def _():
        build_picks()

    real = slice(0, COLS)

    @pl.when(front > 0)
    def _():
        for group in range(GROUPS):
            copy_modal(group, 1).wait_recv()

    def wait_rows(step, carry):
        copy_mode(step, peer_front(step)).wait_recv()
        copy_entry(0, step, peer_front(step)).wait_recv()
        copy_entry(1, step, peer_front(step)).wait_recv()
        return carry

    lax.fori_loop(1, FRONTS, wait_rows, 0)
    projected = dot_last(mode_rows[...], modal[real, :])
    for half in range(2):
        lanes = slice(half * HALF, (half + 1) * HALF)
        flexible = (entries[half] - projected[:, lanes]).astype(BF16)
        rows_out[:, :, lanes] = dot(route[...], flexible).astype(BF16).reshape(SUBS, SHARE, HALF)

    def send_row(step, carry):
        copy_row(step, sub).start()
        return carry

    lax.fori_loop(1, subs, send_row, 0)
    rows_in[sub] = rows_out[sub]

    @pl.when(front == 0)
    def _():
        rows = rows_of(0)
        displaced[rows, :] = dot_wide(back[rows, :], inverse[...])

    def deflate(index, carry):
        columns = chunk(index)
        attachment[:, columns] = (
            displaced[real, columns] - dot(modal[real, :], modes[:, columns])
        ).astype(BF16)
        return carry

    lax.fori_loop(0, CHUNKS, deflate, 0)
    store = pltpu.make_async_copy(attachment, attachment_hbm.at[0], store_sem.at[0])
    store.start()

    def wait_row(step, carry):
        copy_row(step, peer_sub(step)).wait_recv()
        return carry

    lax.fori_loop(1, subs, wait_row, 0)
    high_place = lax.broadcasted_iota(jnp.int32, (SUBS, SHARE, COLS), 0)

    def spread(index, total):
        level = lax.shift_right_logical(ids_ref[pl.ds(index, 1), :], 7)
        chosen = jnp.where(
            high_place == level[:, None, :], rows_in[index].astype(F32)[None, :, :], 0.0
        ).astype(BF16)
        return total + dot_last(chosen.reshape(SUBS * SHARE, COLS), low_pick[index])

    total = lax.fori_loop(0, SUBS, spread, jnp.zeros((SUBS * SHARE, 128), F32))
    for index in range(SUBS):
        flexibility[:, index * 128 : (index + 1) * 128] = total[index * SHARE : (index + 1) * SHARE]
    store_flexibility = pltpu.make_async_copy(flexibility, flexibility_hbm, store_sem.at[1])
    store_flexibility.start()

    for group in range(GROUPS):

        @pl.when(jnp.logical_and(front < last, front >= STARTS[group]))
        def _():
            copy_fwd(group, 0, whole).wait_send()

        @pl.when(front > 0)
        def _():
            copy_bwd(group, 0, whole).wait_send()
            copy_sum(group).wait_send()

        @pl.when(front == 0)
        def _():
            for step in range(1, FRONTS):
                copy_modal(group, step).wait_send()

    def wait_sends(step, carry):
        copy_mode(step, front).wait_send()
        copy_entry(0, step, front).wait_send()
        copy_entry(1, step, front).wait_send()
        return carry

    lax.fori_loop(1, FRONTS, wait_sends, 0)

    def wait_row_sends(step, carry):
        copy_row(step, sub).wait_send()
        return carry

    lax.fori_loop(1, subs, wait_row_sends, 0)
    store.wait()
    store_flexibility.wait()


def on_device(front_inverse, coupling, free_modes, dof_offset, interface_id):
    dma = pltpu.SemaphoreType.DMA
    vmem = pltpu.VMEM
    anywhere = pl.BlockSpec(memory_space=pl.ANY)
    local = pl.BlockSpec(memory_space=pltpu.VMEM)
    return pl.pallas_call(
        kernel,
        out_shape=(
            jax.ShapeDtypeStruct((1, COLS, NF), BF16),
            jax.ShapeDtypeStruct((SHARE, NF), F32),
        ),
        in_specs=[anywhere, anywhere, anywhere, local, local],
        out_specs=(anywhere, anywhere),
        scratch_shapes=[
            vmem((NF, NF), BF16),
            vmem((NF, NF), BF16),
            vmem((MODES, NF), BF16),
            vmem((MPAD, NF), BF16),
            vmem((NF, NF), BF16),
            vmem((NF, NF), BF16),
            vmem((NF, MPAD), BF16),
            vmem((96, NF), F32),
            vmem((OWN, NF), BF16),
            vmem((OWN, NF), BF16),
            vmem((COLS, NF), BF16),
            vmem((COLS, NF), BF16),
            vmem((96, NF), BF16),
            vmem((COLS, NF), BF16),
            vmem((COLS, NF), BF16),
            vmem((COLS, NF), BF16),
            vmem((COLS, MPAD), F32),
            vmem((COLS, MPAD), F32),
            vmem((COLS, MPAD), BF16),
            vmem((COLS, MPAD), BF16),
            vmem((2, COLS, HALF), F32),
            vmem((COLS, COLS), BF16),
            vmem((SUBS, SHARE, COLS), BF16),
            vmem((SUBS, SHARE, COLS), BF16),
            vmem((SUBS, 128, COLS), BF16),
            vmem((COLS, NF), F32),
            vmem((COLS, NF), BF16),
            vmem((SHARE, NF), F32),
            dma((CHUNKS,)),
            dma((CHUNKS,)),
            dma,
            dma((GROUPS,)),
            dma((GROUPS, CHUNKS)),
            dma((GROUPS,)),
            dma((GROUPS, CHUNKS)),
            dma((GROUPS,)),
            dma((GROUPS,)),
            dma((GROUPS, FRONTS)),
            dma((GROUPS,)),
            dma((FRONTS,)),
            dma((FRONTS,)),
            dma((2, FRONTS)),
            dma((2, FRONTS)),
            dma((SUBS,)),
            dma((SUBS,)),
            dma((2,)),
        ],
        compiler_params=pltpu.CompilerParams(
            collective_id=0, has_side_effects=True, vmem_limit_bytes=60 << 20
        ),
        name="chain",
    )(front_inverse, coupling, free_modes, dof_offset, interface_id)


def solution(mesh):
    return jax.shard_map(
        on_device,
        mesh=mesh,
        in_specs=(
            P("sub", "front", None),
            P("sub", "front", None),
            P("sub", None, "front"),
            P("sub", "front"),
            P(),
        ),
        out_specs=(P("sub", None, "front"), P(("sub", "front"), None)),
        check_vma=False,
    )
```

time: 109 us -> 98.7 us (0.906)
  Pallas kernels: 104 us -> 94 us
    pallas_call x1, Pallas kernels: 104 us -> 94 us  [on_device(): pl.pallas_call(kernel, out_shape=(jax.ShapeDtypeStruct((1, COLS, NF), BF1...]
where the time goes in v3:
time: 98.7 us; the launch traced here: 98.5 us
  Pallas kernels  94 us (95%)
  local copies, waits for them, and re-layouts  3.87 us (4%)
    pallas_call x1, Pallas kernels, on_device(): pl.pallas_call(kernel, out_shape=(jax.ShapeDtypeStruct((1, COLS, NF), BF1...  94 us
    unnamed x2, local copies, waits for them, and re-layouts  3.87 us

profile of v3, /device:TPU:32, one launch (start us, length us, event | category | flops | bytes accessed | tf_op | source)
XLA Modules:
  0.0 98.5 jit_solution(18427633341069696520)
XLA Ops:
  0.6 94.0 %chain.1 = (bf16[1,256,2048]{2,1,0:T(8,128)(2,1)}, f32[16,2048]{1,0:T(8,128)}) custom-call(bf16[1,2048,2048]{2,1,0:T(8,128)(2,1)} %inverse_hbm.1, bf16[1,2048,2048]{2,1,0:T(8,128)(2,1)} %coupling_hbm.1, bf16[1,300,2048]{2,1,0:T(8,128)(2,1)} %modes_hbm.1, s32[1,32]{1,0:T(1,128)} %offsets_ref.1, s32[16,256]{1,0:T(8,128)} %ids_ref.1), custom_call_target="tpu_custom_call" | custom-call | tf_op jit(solution)/shard_map/chain/pallas_call | solution.py:593
  94.6 2.3 %copy.9 = bf16[1,256,2048]{2,1,0:T(8,128)(2,1)} copy(bf16[1,256,2048]{2,1,0:T(8,128)(2,1)} %get-tuple-element.4) | data formatting | bytes 2097152
  96.9 1.6 %copy.10 = f32[16,2048]{1,0:T(8,128)} copy(f32[16,2048]{1,0:T(8,128)} %get-tuple-element.5) | data formatting | bytes 262144

commit v4 on v3

--- a/solution.py
+++ b/solution.py
@@ -16,8 +16,8 @@
 NF = 2048
 COLS = 256
 OWN = 32
-STARTS = (0, 1, 3, 5, 8)
-GROUPS = len(STARTS) - 1
+GROUPS = 4
+WIDTH = 64
 CHUNK = 512
 CHUNKS = NF // CHUNK
 MODES = 300
@@ -119,9 +119,6 @@
     load_modes = pltpu.make_async_copy(modes_hbm.at[0], modes_raw, modes_sem)
     for index in range(CHUNKS):
         load_inverse(index).start()
-    for index in range(CHUNKS):
-        load_coupling(index).start()
-    load_modes.start()
 
     def peer_front(step):
         return lax.rem(front + step, FRONTS)
@@ -156,6 +153,7 @@
     def _():
         def one(index, carry):
             load_inverse(index).wait()
+            load_coupling(index).start()
             own[:, chunk(index)] = dot_last(pick[...], inverse[chunk(index), :]).astype(BF16)
             return carry
 
@@ -165,6 +163,7 @@
     def _():
         def one(index, carry):
             load_inverse(index).wait()
+            load_coupling(index).start()
             block = inverse[chunk(index), :].T
             turned[:, chunk(index)] = block
             own[:, chunk(index)] = dot(pick[...], block).astype(BF16)
@@ -172,15 +171,13 @@
 
         lax.fori_loop(0, CHUNKS, one, 0)
 
+    load_modes.start()
     own_rows = pl.ds(pl.multiple_of(front * OWN, OWN), OWN)
     solved[own_rows, :] = own[...]
     pl.semaphore_wait(barrier, FRONTS - 1 + subs - 1)
 
     def rows_of(group):
-        return slice(STARTS[group] * OWN, STARTS[group + 1] * OWN)
-
-    def count_of(group):
-        return (STARTS[group + 1] - STARTS[group]) * OWN
+        return tile(group, WIDTH)
 
     after = jnp.minimum(front + 1, last)
     before = jnp.maximum(front - 1, 0)
@@ -271,7 +268,7 @@
         for index in range(CHUNKS):
             copy_fwd(0, index).start()
 
-    @pl.when(front > 1)
+    @pl.when(front > 0)
     def _():
         def one(index, carry):
             load_coupling(index).wait()
@@ -280,7 +277,7 @@
 
         lax.fori_loop(0, CHUNKS, one, 0)
 
-    @pl.when(front <= 1)
+    @pl.when(front == 0)
     def _():
         def one(index, carry):
             load_coupling(index).wait()
@@ -338,57 +335,37 @@
 
     def forward(group):
         rows = rows_of(group)
-        count = count_of(group)
-        first = STARTS[group]
-        members = STARTS[group + 1] - first
-
-        if group == 0:
-
-            @pl.when(front == 1)
-            def _():
-                for index in range(CHUNKS):
-                    columns = chunk_lanes(index)
-                    copy_fwd(group, index).wait_recv()
-                    part = dot_last(solved_in[rows, columns], coupling[:, columns])
-                    gathered[:count] = part if index == 0 else gathered[:count] + part
-                reduced[:count] = gathered[:count].astype(BF16)
-
-        @pl.when(front > max(first, 1))
+
+        @pl.when(front > 2 * group)
         def _():
             for index in range(CHUNKS):
                 columns = chunk_lanes(index)
                 copy_fwd(group, index).wait_recv()
                 part = dot_wide(solved_in[rows, columns], coupling_turned[columns, :])
                 if index == 0:
-                    gathered[:count] = part
+                    gathered[...] = part
                 elif index < CHUNKS - 1:
-                    gathered[:count] = gathered[:count] + part
+                    gathered[...] = gathered[...] + part
                 else:
-                    reduced[:count] = (gathered[:count] + part).astype(BF16)
-
-        @pl.when(front > first)
-        def _():
+                    reduced[...] = (gathered[...] + part).astype(BF16)
+
+            first = tile(2 * group, OWN)
+            second = tile(2 * group + 1, OWN)
             for index in range(CHUNKS):
                 columns = chunk_lanes(index)
-                result = (0.0 - dot_wide(reduced[:count], turned[:, columns])).astype(BF16)
-                solved[first * OWN : (first + 1) * OWN, columns] = result[:OWN]
-                for member in range(1, members):
-
-                    @pl.when(front > first + member)
-                    def _():
-                        part = slice(member * OWN, (member + 1) * OWN)
-                        solved[(first + member) * OWN : (first + member + 1) * OWN, columns] = result[part]
+                result = 0.0 - dot_wide(reduced[...], turned[:, columns])
+                solved[first, columns] = result[:OWN].astype(BF16)
+                kept = solved[second, columns].astype(F32)
+                solved[second, columns] = jnp.where(front == 2 * group + 1, kept, result[OWN:]).astype(BF16)
 
                 @pl.when(front < last)
                 def _():
                     copy_fwd(group, index).start()
 
-        if group > 0:
-
-            @pl.when(front == first)
-            def _():
-                for index in range(CHUNKS):
-                    copy_fwd(group, index).start()
+        @pl.when(jnp.logical_and(front == 2 * group, front > 0))
+        def _():
+            for index in range(CHUNKS):
+                copy_fwd(group, index).start()
 
     def send_entries(half):
         columns = pl.ds(half * HALF, HALF)
@@ -398,20 +375,16 @@
 
     def backward(group):
         rows = rows_of(group)
-        count = count_of(group)
         for index in range(CHUNKS):
             columns = chunk_lanes(index)
 
             @pl.when(front < last)
             def _():
                 copy_bwd(group, index).wait_recv()
-                back[rows, columns] = (
-                    solved[rows, columns].astype(F32) - handed_in[rows, columns].astype(F32)
-                ).astype(BF16)
-
-            @pl.when(front == last)
-            def _():
-                back[rows, columns] = solved[rows, columns]
+
+            upper = solved[rows, columns].astype(F32)
+            lower = handed_in[rows, columns].astype(F32)
+            back[rows, columns] = jnp.where(front == last, upper, upper - lower).astype(BF16)
 
             @pl.when(front > 0)
             def _():
@@ -420,7 +393,7 @@
                     total = displaced[rows, :] + total
                 displaced[rows, :] = total
                 if index == CHUNKS - 1:
-                    reduced[:count] = total.astype(BF16)
+                    reduced[...] = total.astype(BF16)
 
             @pl.when(front == 0)
             def _():
@@ -431,10 +404,10 @@
         def _():
             for index in range(CHUNKS):
                 columns = chunk_lanes(index)
-                handed[rows, columns] = dot_wide(reduced[:count], coupling[:, columns]).astype(BF16)
+                handed[rows, columns] = dot_wide(reduced[...], coupling[:, columns]).astype(BF16)
                 copy_bwd(group, index).start()
 
-            modal_out[rows, :] = dot_wide(reduced[:count], modal_map[...])
+            modal_out[rows, :] = dot_wide(reduced[...], modal_map[...])
 
         @pl.when(front < last)
         def _():
@@ -450,14 +423,16 @@
             modal[rows, :] = modal_out[rows, :].astype(BF16)
             for step in (4, 5, 3, 2, 6, 7, 1):
                 copy_modal(group, step).start()
-            if group > 0:
-                displaced[rows, :] = dot_wide(back[rows, :], inverse[...])
-
-        if group == 2:
+
+        @pl.when(group == 2)
+        def _():
             send_entries(1)
 
-    build_modal_at = jnp.where(front < 2, 5, 0)
+    build_modal_at = jnp.where(
+        front < 5, jnp.maximum(2 * front + 1, 5), jnp.where(front < last, 1, 0)
+    )
     build_picks_at = jnp.where(front < 4, 9, 99)
+    shift = jnp.where(front == last, 1, -1)
 
     def slot(moment, carry):
         @pl.when(moment == build_modal_at)
@@ -468,17 +443,24 @@
         def _():
             build_picks()
 
-        for group in range(GROUPS):
-            turn_f = 2 * (front - STARTS[group])
-            turn_b = 2 * (15 - STARTS[group] - front) + jnp.where(front >= last - 1, -1, 1)
-
-            @pl.when(moment == turn_f)
-            def _():
-                forward(group)
-
-            @pl.when(moment == turn_b)
-            def _():
-                backward(group)
+        even = lax.rem(moment, 2) == 0
+        ahead = front - moment // 2
+        behind = 15 - front - (moment + shift) // 2
+
+        @pl.when(jnp.logical_and(even, jnp.logical_and(ahead >= 0, lax.rem(ahead + 32, 2) == 0)))
+        def _():
+            forward(ahead // 2)
+
+        @pl.when(
+            jnp.logical_and(
+                jnp.logical_not(even),
+                jnp.logical_and(
+                    jnp.logical_and(behind >= 0, behind < 2 * GROUPS), lax.rem(behind + 32, 2) == 0
+                ),
+            )
+        )
+        def _():
+            backward(behind // 2)
 
         return carry
 
@@ -518,8 +500,12 @@
 
     @pl.when(front == 0)
     def _():
-        rows = rows_of(0)
-        displaced[rows, :] = dot_wide(back[rows, :], inverse[...])
+        def displace(index, carry):
+            columns = chunk(index)
+            displaced[:, columns] = dot(back[...], inverse[:, columns])
+            return carry
+
+        lax.fori_loop(0, CHUNKS, displace, 0)
 
     def deflate(index, carry):
         columns = chunk(index)
@@ -532,21 +518,17 @@
     store = pltpu.make_async_copy(attachment, attachment_hbm.at[0], store_sem.at[0])
     store.start()
 
-    def wait_row(step, carry):
-        copy_row(step, peer_sub(step)).wait_recv()
-        return carry
-
-    lax.fori_loop(1, subs, wait_row, 0)
     high_place = lax.broadcasted_iota(jnp.int32, (SUBS, SHARE, COLS), 0)
-
-    def spread(index, total):
-        level = lax.shift_right_logical(ids_ref[pl.ds(index, 1), :], 7)
+    total = jnp.zeros((SUBS * SHARE, 128), F32)
+    for step in range(subs):
+        source = peer_sub(step)
+        if step > 0:
+            copy_row(step, source).wait_recv()
+        level = lax.shift_right_logical(ids_ref[pl.ds(source, 1), :], 7)
         chosen = jnp.where(
-            high_place == level[:, None, :], rows_in[index].astype(F32)[None, :, :], 0.0
+            high_place == level[:, None, :], rows_in[source].astype(F32)[None, :, :], 0.0
         ).astype(BF16)
-        return total + dot_last(chosen.reshape(SUBS * SHARE, COLS), low_pick[index])
-
-    total = lax.fori_loop(0, SUBS, spread, jnp.zeros((SUBS * SHARE, 128), F32))
+        total = total + dot_last(chosen.reshape(SUBS * SHARE, COLS), low_pick[source])
     for index in range(SUBS):
         flexibility[:, index * 128 : (index + 1) * 128] = total[index * SHARE : (index + 1) * SHARE]
     store_flexibility = pltpu.make_async_copy(flexibility, flexibility_hbm, store_sem.at[1])
@@ -554,7 +536,7 @@
 
     for group in range(GROUPS):
 
-        @pl.when(jnp.logical_and(front < last, front >= STARTS[group]))
+        @pl.when(jnp.logical_and(front < last, front >= 2 * group))
         def _():
             copy_fwd(group, 0, whole).wait_send()
 
@@ -606,12 +588,12 @@
             vmem((NF, NF), BF16),
             vmem((NF, NF), BF16),
             vmem((NF, MPAD), BF16),
-            vmem((96, NF), F32),
+            vmem((WIDTH, NF), F32),
             vmem((OWN, NF), BF16),
             vmem((OWN, NF), BF16),
             vmem((COLS, NF), BF16),
             vmem((COLS, NF), BF16),
-            vmem((96, NF), BF16),
+            vmem((WIDTH, NF), BF16),
             vmem((COLS, NF), BF16),
             vmem((COLS, NF), BF16),
             vmem((COLS, NF), BF16),

time: 98.7 us -> 96.1 us (0.974)
  Pallas kernels: 94 us -> 91.4 us
    pallas_call x1, Pallas kernels: 94 us -> 91.4 us  [on_device(): pl.pallas_call(kernel, out_shape=(jax.ShapeDtypeStruct((1, COLS, NF), BF1...]
where the time goes in v4:
time: 96.1 us; the launch traced here: 95.9 us
  Pallas kernels  91.4 us (95%)
  local copies, waits for them, and re-layouts  3.87 us (4%)
    pallas_call x1, Pallas kernels, on_device(): pl.pallas_call(kernel, out_shape=(jax.ShapeDtypeStruct((1, COLS, NF), BF1...  91.4 us
    unnamed x2, local copies, waits for them, and re-layouts  3.87 us

profile of v4, /device:TPU:32, one launch (start us, length us, event | category | flops | bytes accessed | tf_op | source)
XLA Modules:
  0.0 95.9 jit_solution(883400999019375907)
XLA Ops:
  0.6 91.4 %chain.1 = (bf16[1,256,2048]{2,1,0:T(8,128)(2,1)}, f32[16,2048]{1,0:T(8,128)}) custom-call(bf16[1,2048,2048]{2,1,0:T(8,128)(2,1)} %inverse_hbm.1, bf16[1,2048,2048]{2,1,0:T(8,128)(2,1)} %coupling_hbm.1, bf16[1,300,2048]{2,1,0:T(8,128)(2,1)} %modes_hbm.1, s32[1,32]{1,0:T(1,128)} %offsets_ref.1, s32[16,256]{1,0:T(8,128)} %ids_ref.1), custom_call_target="tpu_custom_call" | custom-call | tf_op jit(solution)/shard_map/chain/pallas_call | solution.py:575
  92.0 2.3 %copy.9 = bf16[1,256,2048]{2,1,0:T(8,128)(2,1)} copy(bf16[1,256,2048]{2,1,0:T(8,128)(2,1)} %get-tuple-element.4) | data formatting | bytes 2097152
  94.3 1.6 %copy.10 = f32[16,2048]{1,0:T(8,128)} copy(f32[16,2048]{1,0:T(8,128)} %get-tuple-element.5) | data formatting | bytes 262144

commit v5 on v4

--- a/solution.py
+++ b/solution.py
@@ -78,6 +78,7 @@
     rows_out,
     rows_in,
     low_pick,
+    placed,
     displaced,
     attachment,
     flexibility,
@@ -328,7 +329,7 @@
 
         def fill_low(index, carry):
             ids = jnp.bitwise_and(ids_ref[pl.ds(index, 1), :], 127)
-            low_pick[index] = (lane_place == ids).astype(F32).astype(BF16)
+            low_pick[:, tile(index, COLS)] = (lane_place == ids).astype(F32).astype(BF16)
             return carry
 
         lax.fori_loop(0, SUBS, fill_low, 0)
@@ -373,6 +374,16 @@
         for step in (4, 5, 3, 2, 6, 7, 1):
             copy_entry(half, step, front).start()
 
+    def displace_rows(group):
+        rows = rows_of(group)
+
+        def one(index, carry):
+            columns = tile(index, 2 * CHUNK)
+            displaced[rows, columns] = dot_wide(back[rows, :], inverse[:, columns])
+            return carry
+
+        lax.fori_loop(0, CHUNKS // 2, one, 0)
+
     def backward(group):
         rows = rows_of(group)
         for index in range(CHUNKS):
@@ -424,6 +435,10 @@
             for step in (4, 5, 3, 2, 6, 7, 1):
                 copy_modal(group, step).start()
 
+        @pl.when(jnp.logical_and(front == 0, group > 0))
+        def _():
+            displace_rows(group)
+
         @pl.when(group == 2)
         def _():
             send_entries(1)
@@ -467,6 +482,10 @@
     lax.fori_loop(0, 32, slot, 0)
     send_entries(0)
 
+    @pl.when(front == 0)
+    def _():
+        displace_rows(0)
+
     @pl.when(front >= 4)
     def _():
         build_picks()
@@ -498,15 +517,6 @@
     lax.fori_loop(1, subs, send_row, 0)
     rows_in[sub] = rows_out[sub]
 
-    @pl.when(front == 0)
-    def _():
-        def displace(index, carry):
-            columns = chunk(index)
-            displaced[:, columns] = dot(back[...], inverse[:, columns])
-            return carry
-
-        lax.fori_loop(0, CHUNKS, displace, 0)
-
     def deflate(index, carry):
         columns = chunk(index)
         attachment[:, columns] = (
@@ -518,17 +528,19 @@
     store = pltpu.make_async_copy(attachment, attachment_hbm.at[0], store_sem.at[0])
     store.start()
 
+    def wait_row(step, carry):
+        copy_row(step, peer_sub(step)).wait_recv()
+        return carry
+
+    lax.fori_loop(1, subs, wait_row, 0)
     high_place = lax.broadcasted_iota(jnp.int32, (SUBS, SHARE, COLS), 0)
-    total = jnp.zeros((SUBS * SHARE, 128), F32)
-    for step in range(subs):
-        source = peer_sub(step)
-        if step > 0:
-            copy_row(step, source).wait_recv()
-        level = lax.shift_right_logical(ids_ref[pl.ds(source, 1), :], 7)
+    for index in range(SUBS):
+        level = lax.shift_right_logical(ids_ref[index : index + 1, :], 7)
         chosen = jnp.where(
-            high_place == level[:, None, :], rows_in[source].astype(F32)[None, :, :], 0.0
+            high_place == level[:, None, :], rows_in[index].astype(F32)[None, :, :], 0.0
         ).astype(BF16)
-        total = total + dot_last(chosen.reshape(SUBS * SHARE, COLS), low_pick[source])
+        placed[:, index * COLS : (index + 1) * COLS] = chosen.reshape(SUBS * SHARE, COLS)
+    total = dot_last(placed[...], low_pick[...])
     for index in range(SUBS):
         flexibility[:, index * 128 : (index + 1) * 128] = total[index * SHARE : (index + 1) * SHARE]
     store_flexibility = pltpu.make_async_copy(flexibility, flexibility_hbm, store_sem.at[1])
@@ -605,7 +617,8 @@
             vmem((COLS, COLS), BF16),
             vmem((SUBS, SHARE, COLS), BF16),
             vmem((SUBS, SHARE, COLS), BF16),
-            vmem((SUBS, 128, COLS), BF16),
+            vmem((128, SUBS * COLS), BF16),
+            vmem((SUBS * SHARE, SUBS * COLS), BF16),
             vmem((COLS, NF), F32),
             vmem((COLS, NF), BF16),
             vmem((SHARE, NF), F32),

time: 96.1 us -> 96.1 us (level)
  no operation moved by 1% of the time
where the time goes in v5:
time: 96.1 us; the launch traced here: 95.9 us
  Pallas kernels  91.4 us (95%)
  local copies, waits for them, and re-layouts  3.87 us (4%)
    pallas_call x1, Pallas kernels, on_device(): pl.pallas_call(kernel, out_shape=(jax.ShapeDtypeStruct((1, COLS, NF), BF1...  91.4 us
    unnamed x2, local copies, waits for them, and re-layouts  3.87 us

profile of v5, /device:TPU:32, one launch (start us, length us, event | category | flops | bytes accessed | tf_op | source)
XLA Modules:
  0.0 95.9 jit_solution(15882601308233329976)
XLA Ops:
  0.6 91.4 %chain.1 = (bf16[1,256,2048]{2,1,0:T(8,128)(2,1)}, f32[16,2048]{1,0:T(8,128)}) custom-call(bf16[1,2048,2048]{2,1,0:T(8,128)(2,1)} %inverse_hbm.1, bf16[1,2048,2048]{2,1,0:T(8,128)(2,1)} %coupling_hbm.1, bf16[1,300,2048]{2,1,0:T(8,128)(2,1)} %modes_hbm.1, s32[1,32]{1,0:T(1,128)} %offsets_ref.1, s32[16,256]{1,0:T(8,128)} %ids_ref.1), custom_call_target="tpu_custom_call" | custom-call | tf_op jit(solution)/shard_map/chain/pallas_call | solution.py:587
  92.0 2.3 %copy.9 = bf16[1,256,2048]{2,1,0:T(8,128)(2,1)} copy(bf16[1,256,2048]{2,1,0:T(8,128)(2,1)} %get-tuple-element.4) | data formatting | bytes 2097152
  94.3 1.6 %copy.10 = f32[16,2048]{1,0:T(8,128)} copy(f32[16,2048]{1,0:T(8,128)} %get-tuple-element.5) | data formatting | bytes 262144

commit v6 on v5

--- a/solution.py
+++ b/solution.py
@@ -70,6 +70,7 @@
     handed,
     handed_in,
     modal_out,
+    modal_part,
     modal_in,
     modal,
     mode_rows,
@@ -211,7 +212,7 @@
 
     def copy_sum(group):
         return pltpu.make_async_remote_copy(
-            src_ref=modal_out.at[rows_of(group)],
+            src_ref=modal_part.at[rows_of(group)],
             dst_ref=modal_in.at[rows_of(group)],
             send_sem=sum_send.at[group],
             recv_sem=sum_recv.at[group],
@@ -423,10 +424,11 @@
         @pl.when(front < last)
         def _():
             copy_sum(group).wait_recv()
-            modal_out[rows, :] = modal_out[rows, :] + modal_in[rows, :]
+            modal_out[rows, :] = modal_out[rows, :] + modal_in[rows, :].astype(F32)
 
         @pl.when(front > 0)
         def _():
+            modal_part[rows, :] = modal_out[rows, :].astype(BF16)
             copy_sum(group).start()
 
         @pl.when(front == 0)
@@ -610,7 +612,8 @@
             vmem((COLS, NF), BF16),
             vmem((COLS, NF), BF16),
             vmem((COLS, MPAD), F32),
-            vmem((COLS, MPAD), F32),
+            vmem((COLS, MPAD), BF16),
+            vmem((COLS, MPAD), BF16),
             vmem((COLS, MPAD), BF16),
             vmem((COLS, MPAD), BF16),
             vmem((2, COLS, HALF), F32),

time: 96.1 us -> 96.3 us (level)
  no operation moved by 1% of the time
where the time goes in v6:
time: 96.3 us; the launch traced here: 96.1 us
  Pallas kernels  91.6 us (95%)
  local copies, waits for them, and re-layouts  3.87 us (4%)
    pallas_call x1, Pallas kernels, on_device(): pl.pallas_call(kernel, out_shape=(jax.ShapeDtypeStruct((1, COLS, NF), BF1...  91.6 us
    unnamed x2, local copies, waits for them, and re-layouts  3.87 us

profile of v6, /device:TPU:32, one launch (start us, length us, event | category | flops | bytes accessed | tf_op | source)
XLA Modules:
  0.0 96.1 jit_solution(8324499832080405793)
XLA Ops:
  0.6 91.6 %chain.1 = (bf16[1,256,2048]{2,1,0:T(8,128)(2,1)}, f32[16,2048]{1,0:T(8,128)}) custom-call(bf16[1,2048,2048]{2,1,0:T(8,128)(2,1)} %inverse_hbm.1, bf16[1,2048,2048]{2,1,0:T(8,128)(2,1)} %coupling_hbm.1, bf16[1,300,2048]{2,1,0:T(8,128)(2,1)} %modes_hbm.1, s32[1,32]{1,0:T(1,128)} %offsets_ref.1, s32[16,256]{1,0:T(8,128)} %ids_ref.1), custom_call_target="tpu_custom_call" | custom-call | tf_op jit(solution)/shard_map/chain/pallas_call | solution.py:589
  92.2 2.3 %copy.9 = bf16[1,256,2048]{2,1,0:T(8,128)(2,1)} copy(bf16[1,256,2048]{2,1,0:T(8,128)(2,1)} %get-tuple-element.4) | data formatting | bytes 2097152
  94.5 1.6 %copy.10 = f32[16,2048]{1,0:T(8,128)} copy(f32[16,2048]{1,0:T(8,128)} %get-tuple-element.5) | data formatting | bytes 262144
